TPU v7x, 32 devices: a whole 2x2x4 slice. The times are simulated.
32 devices in a mesh: lat: 8 (over z, y), lon: 4 (over x, core).
Axes of the slice: x: 2, y: 2, z: 4, core: 2. Of those that a mesh axis runs over, the one named last changes fastest.
Arguments:
- pair_table: int32 [640], replicated, may hold values from 0 to 639, each once
- spectral: bfloat16 [640, 384, 1408], P('lat', 'lon'), may hold values from -0.071777344 to 0.071777344
- lat_basis: bfloat16 [640, 32, 1408], P('lat'), may hold values from -0.15625 to 0.15625
- in_weight: bfloat16 [192, 512], replicated, may hold values from -0.4375 to 0.4375
- in_bias: float32 [512], replicated, may hold values from -3 to 3
- out_weight: bfloat16 [512, 192], replicated, may hold values from -0.25 to 0.25
- out_bias: float32 [192], replicated, may hold values from -3 to 3
- cotangent: bfloat16 [64, 192, 2560], P('lat', None, 'lon'), may hold values from -0.08984375 to 0.08984375
Outputs:
- tendency: bfloat16 [64, 192, 2560], P('lat', None, 'lon')
- spectral_grad: bfloat16 [640, 384, 1408], P('lat', 'lon')
- in_weight_grad: float32 [192, 512], replicated
- in_bias_grad: float32 [512], replicated
- out_weight_grad: float32 [512, 192], replicated
- out_bias_grad: float32 [192], replicated
Inputs may be any that keep to these rules, and one draw needn't show every extreme that they name: `pair_table`: each pair number appears exactly once.
All inputs are finite; a program needn't handle non-finite values.
Results may differ from a plain program's by a relative error of at most 0.015.
Values may be sent and summed in bfloat16 or wider, within the bound.
No kernel may reach another device: no remote copies, remote signals or barrier semaphores. Data moves between devices by JAX's collectives and lax.ppermute only.
A program may use at most 256 MiB of HBM per device.

v0:
```python
import math

import jax
import jax.numpy as jnp
from jax import lax
from jax.experimental import pallas as pl
from jax.experimental.pallas import tpu as pltpu
from jax.sharding import PartitionSpec as P

TRUNC = 1279


def pair_masks(pair_ids, length):
    first_len = TRUNC + 1 - pair_ids
    position = jnp.arange(length, dtype=jnp.int32)[None, :]
    lower_part = position < first_len[:, None]
    upper_part = jnp.logical_and(position >= first_len[:, None], position < TRUNC + 2)
    offset = jnp.where(lower_part, position, position - first_len[:, None])
    parity = jnp.where(offset % 2 == 0, 1.0, -1.0).astype(jnp.float32)
    return (lower_part, upper_part, parity, first_len)


def wave_numbers(pair_ids):
    both = jnp.stack([pair_ids, TRUNC - pair_ids], axis=1)
    return both.reshape(-1)


def table_kernel(cos_a_ref, sin_a_ref, cos_b_ref, sin_b_ref, factor_ref, out_ref):
    fine = cos_b_ref.shape[1]
    cos_b = cos_b_ref[...]
    sin_b = sin_b_ref[...]
    factor = factor_ref[...]
    for u in range(cos_a_ref.shape[1]):
        cos_a = cos_a_ref[:, u : u + 1]
        sin_a = sin_a_ref[:, u : u + 1]
        cols = slice(u * fine, (u + 1) * fine)
        out_ref[0, :, cols] = (factor * (cos_a * cos_b - sin_a * sin_b)).astype(out_ref.dtype)
        out_ref[1, :, cols] = (-factor * (sin_a * cos_b + cos_a * sin_b)).astype(out_ref.dtype)


def fourier_table(numbers, lon_total):
    fine = 128
    count = numbers.shape[0]
    coarse = jnp.arange(lon_total // fine, dtype=jnp.int32) * fine
    scale = 2.0 * math.pi / lon_total

    def angles(offsets):
        phase = numbers[:, None] * offsets[None, :] % lon_total
        angle = phase.astype(jnp.float32) * scale
        return jnp.cos(angle), jnp.sin(angle)

    cos_a, sin_a = angles(coarse)
    cos_b, sin_b = angles(jnp.arange(fine, dtype=jnp.int32))
    factor = jnp.where(numbers == 0, 1.0, 2.0).astype(jnp.float32)[:, None]
    rows = 128 if count % 128 == 0 else count
    return pl.pallas_call(
        table_kernel,
        grid=(count // rows,),
        in_specs=[
            pl.BlockSpec((rows, coarse.shape[0]), lambda i: (i, 0)),
            pl.BlockSpec((rows, coarse.shape[0]), lambda i: (i, 0)),
            pl.BlockSpec((rows, fine), lambda i: (i, 0)),
            pl.BlockSpec((rows, fine), lambda i: (i, 0)),
            pl.BlockSpec((rows, 1), lambda i: (i, 0)),
        ],
        out_specs=pl.BlockSpec((2, rows, lon_total), lambda i: (0, i, 0)),
        out_shape=jax.ShapeDtypeStruct((2, count, lon_total), jnp.bfloat16),
    )(cos_a, sin_a, cos_b, sin_b, factor)


def all_reduce(value, axes):
    count = 1
    for name in axes:
        count *= lax.axis_size(name)
    flat = value.reshape(-1)
    chunk = -(-flat.shape[0] // (count * 128)) * 128
    flat = jnp.pad(flat, (0, chunk * count - flat.shape[0]))
    parts = lax.all_to_all(flat.reshape(count, chunk), axes, 0, 0, tiled=True)
    owned = jnp.sum(parts, axis=0, keepdims=True)
    spread = jnp.broadcast_to(owned, (count, chunk))
    whole = lax.all_to_all(spread, axes, 0, 0, tiled=True).reshape(-1)
    return whole[: value.size].reshape(value.shape)


def masked_rows(ids_ref, pair_index, basis, rows_ref):
    half, length = basis.shape
    pair = ids_ref[pair_index]
    first = TRUNC + 1 - pair
    position = lax.broadcasted_iota(jnp.int32, (1, length), 1)
    lower = position < first
    upper = jnp.logical_and(position >= first, position < TRUNC + 2)
    offset = jnp.where(lower, position, position - first)
    odd = offset % 2 == 1
    zero = jnp.zeros_like(basis)
    signed = jnp.where(odd, -basis, basis)
    rows_ref[0:half, :] = jnp.where(lower, basis, zero)
    rows_ref[half : 2 * half, :] = jnp.where(lower, signed, zero)
    rows_ref[2 * half : 3 * half, :] = jnp.where(upper, basis, zero)
    rows_ref[3 * half : 4 * half, :] = jnp.where(upper, signed, zero)


def synth_kernel(ids_ref, spec_ref, basis_ref, out_ref, rows_ref):
    block = basis_ref.shape[0]
    step = pl.program_id(0)
    for i in range(block):
        masked_rows(ids_ref, step * block + i, basis_ref[i], rows_ref)
        out = lax.dot_general(
            rows_ref[...], spec_ref[i], (((1,), (1,)), ((), ())),
            preferred_element_type=jnp.float32,
        )
        out_ref[i] = out.astype(out_ref.dtype)


def analyse_kernel(ids_ref, grad_ref, basis_ref, out_ref, rows_ref):
    block = basis_ref.shape[0]
    step = pl.program_id(0)
    for i in range(block):
        masked_rows(ids_ref, step * block + i, basis_ref[i], rows_ref)
        out = jnp.dot(grad_ref[i], rows_ref[...], preferred_element_type=jnp.float32)
        out_ref[i] = out.astype(out_ref.dtype)


def pair_block(count):
    for size in (8, 4, 2, 1):
        if count % size == 0:
            return size


def synthesis(local_ids, spectral, lat_basis):
    pairs, width, length = spectral.shape
    half = lat_basis.shape[1]
    block = pair_block(pairs)
    spec = pltpu.PrefetchScalarGridSpec(
        num_scalar_prefetch=1,
        grid=(pairs // block,),
        in_specs=[
            pl.BlockSpec((block, width, length), lambda s, ids: (s, 0, 0)),
            pl.BlockSpec((block, half, length), lambda s, ids: (s, 0, 0)),
        ],
        out_specs=pl.BlockSpec((block, 4 * half, width), lambda s, ids: (s, 0, 0)),
        scratch_shapes=[pltpu.VMEM((4 * half, length), lat_basis.dtype)],
    )
    return pl.pallas_call(
        synth_kernel,
        grid_spec=spec,
        out_shape=jax.ShapeDtypeStruct((pairs, 4 * half, width), jnp.bfloat16),
    )(local_ids, spectral, lat_basis)


def analysis(local_ids, grads, lat_basis):
    pairs, width, rows = grads.shape
    half, length = lat_basis.shape[1], lat_basis.shape[2]
    block = pair_block(pairs)
    spec = pltpu.PrefetchScalarGridSpec(
        num_scalar_prefetch=1,
        grid=(pairs // block,),
        in_specs=[
            pl.BlockSpec((block, width, rows), lambda s, ids: (s, 0, 0)),
            pl.BlockSpec((block, half, length), lambda s, ids: (s, 0, 0)),
        ],
        out_specs=pl.BlockSpec((block, width, length), lambda s, ids: (s, 0, 0)),
        scratch_shapes=[pltpu.VMEM((4 * half, length), lat_basis.dtype)],
    )
    return pl.pallas_call(
        analyse_kernel,
        grid_spec=spec,
        out_shape=jax.ShapeDtypeStruct((pairs, width, length), jnp.bfloat16),
    )(local_ids, grads, lat_basis)


def per_device(
    pair_table, spectral, lat_basis, in_weight, in_bias, out_weight, out_bias, cotangent
):
    pair_dev = spectral.shape[0]
    width_local = spectral.shape[1]
    lat_half = lat_basis.shape[1]
    band_rows = cotangent.shape[0]
    block_cols = cotangent.shape[2]
    lon_total = block_cols * lax.axis_size("lon")
    first_row = lax.axis_index("lat") * pair_dev
    local_ids = lax.dynamic_slice_in_dim(pair_table, first_row, pair_dev)
    lat_window = 2 * lat_half
    raw_waves = synthesis(local_ids, spectral, lat_basis).reshape(
        pair_dev, 2, lat_window, width_local
    )
    waves = jnp.concatenate(
        [raw_waves[:, :, :lat_half], jnp.flip(raw_waves[:, :, lat_half:], axis=2)], axis=2
    )
    flat_waves = waves.reshape(2 * pair_dev, lat_window * width_local)
    band_waves = lax.all_to_all(flat_waves, "lat", split_axis=1, concat_axis=0, tiled=True)
    wave_count = band_waves.shape[0]
    coeff_grid = band_waves.reshape(wave_count, band_rows, width_local // 2, 2)
    numbers = wave_numbers(pair_table)
    full_table = fourier_table(numbers, lon_total)
    all_columns = jnp.einsum(
        "glkc,cgn->lkn", coeff_grid, full_table, preferred_element_type=jnp.float32
    ).astype(jnp.bfloat16)
    grid = lax.all_to_all(all_columns, "lon", split_axis=2, concat_axis=1, tiled=True)
    pre_act = (
        jnp.einsum("lkc,kh->lch", grid, in_weight, preferred_element_type=jnp.float32) + in_bias
    )
    activated, gelu_back = jax.vjp(jax.nn.gelu, pre_act)
    hidden = activated.astype(jnp.bfloat16)
    tendency = (
        jnp.einsum("lch,hk->lkc", hidden, out_weight, preferred_element_type=jnp.float32)
        + out_bias[None, :, None]
    ).astype(jnp.bfloat16)
    out_weight_part = jnp.einsum(
        "lch,lkc->kh", hidden, cotangent, preferred_element_type=jnp.float32
    )
    out_bias_part = jnp.sum(cotangent.astype(jnp.float32), axis=(0, 2))
    hidden_grad = jnp.einsum(
        "lkc,hk->lch", cotangent, out_weight, preferred_element_type=jnp.float32
    )
    pre_grad = gelu_back(hidden_grad)[0].astype(jnp.bfloat16)
    in_weight_part = jnp.einsum("lkc,lch->kh", grid, pre_grad, preferred_element_type=jnp.float32)
    in_bias_part = jnp.sum(pre_grad.astype(jnp.float32), axis=(0, 1))
    grid_grad = jnp.einsum(
        "lch,kh->lkc", pre_grad, in_weight, preferred_element_type=jnp.float32
    ).astype(jnp.bfloat16)
    channels, hid = in_weight.shape
    width = max(hid, channels)

    def widen(v):
        return jnp.pad(v, ((0, 0), (0, width - v.shape[1])))

    stacked = jnp.concatenate(
        [
            widen(in_weight_part),
            widen(out_weight_part),
            widen(in_bias_part[None, :]),
            widen(out_bias_part[None, :]),
        ],
        axis=0,
    )
    summed = all_reduce(stacked, ("lat", "lon"))
    in_weight_grad = summed[:channels, :hid]
    out_weight_grad = summed[channels : 2 * channels, :hid].T
    in_bias_grad = summed[2 * channels, :hid]
    out_bias_grad = summed[2 * channels + 1, :channels]
    level_rows = lax.all_to_all(grid_grad, "lon", split_axis=1, concat_axis=2, tiled=True)
    wave_grad = jnp.einsum(
        "cgn,lkn->glkc", full_table, level_rows, preferred_element_type=jnp.float32
    ).astype(jnp.bfloat16)
    flat_grad = wave_grad.reshape(wave_count, band_rows * width_local)
    pair_grad = lax.all_to_all(flat_grad, "lat", split_axis=0, concat_axis=1, tiled=True)
    pair_grad = pair_grad.reshape(pair_dev, 2, lat_window, width_local)
    pair_grad = jnp.concatenate(
        [pair_grad[:, :, :lat_half], jnp.flip(pair_grad[:, :, lat_half:], axis=2)], axis=2
    )
    pair_grad = jnp.swapaxes(pair_grad.reshape(pair_dev, 2 * lat_window, width_local), 1, 2)
    spectral_grad = analysis(local_ids, pair_grad, lat_basis)
    return (tendency, spectral_grad, in_weight_grad, in_bias_grad, out_weight_grad, out_bias_grad)


def solution(mesh):
    placed = (
        P(),
        P("lat", "lon", None),
        P("lat", None, None),
        P(),
        P(),
        P(),
        P(),
        P("lat", None, "lon"),
    )
    return jax.shard_map(
        per_device,
        mesh=mesh,
        in_specs=placed,
        out_specs=(P("lat", None, "lon"), P("lat", "lon", None), P(), P(), P(), P()),
        check_vma=False,
    )
```

profile of v0, /device:TPU:0, one launch (start us, length us, event | category | flops | bytes accessed | tf_op | source)
XLA Modules:
  0.0 350.7 jit_solution(15890510725770249304)
XLA Ops:
  2.0 17.1 %shard_map.127 = bf16[80,128,96]{2,1,0:T(8,128)(2,1)} custom-call(s32[80]{0:T(128)} %dynamic_slice.3.ids_ref, bf16[80,96,1408]{2,1,0:T(8,128)(2,1)} %spec_ref.1, bf16[80,32,1408]{2,1,0:T(8,128)(2,1)} %basis_ref.3), custom_call_target="tpu_custom_call" | custom-call | tf_op jit(solution)/shard_map/pallas_call | solution.py:143
  33.9 7.8 %all-to-all-start = ((bf16[160,8,768]{2,0,1:T(8,128)(2,1)}), bf16[160,8,768]{2,0,1:T(8,128)(2,1)S(1)}, u32[]{:S(2)}, u32[]{:S(2)}) async-start(bf16[160,8,768]{2,0,1:T(8,128)(2,1)} %copy.78), calls=%async_computation | async-start | bytes 3932160 | tf_op jit(solution)/shard_map/all_to_all | solution.py:190
  51.0 12.7 %shard_map.128 = bf16[2,1280,2560]{2,1,0:T(8,128)(2,1)} custom-call(f32[1280,20]{1,0:T(8,128)} %get-tuple-element.13.cos_a_ref, f32[1280,20]{1,0:T(8,128)} %get-tuple-element.12.sin_a_ref, f32[1280,128]{1,0:T(8,128)} %get-tuple-element.15.cos_b_ref, f32[1280,128]{1,0:T(8,128)} %get-tuple-element.14.sin_b_ref, f32[1280,1]{1,0:T(8,128)} %select_n.35.factor_ref), custom_call_target="tpu_custom_call" | custom-call | tf_op jit(solution)/shard_map/pallas_call | solution.py:56
  63.7 23.4 %all-to-all-done = bf16[160,8,768]{2,0,1:T(8,128)(2,1)S(1)} async-done(((bf16[160,8,768]{2,0,1:T(8,128)(2,1)}), bf16[160,8,768]{2,0,1:T(8,128)(2,1)S(1)}, u32[]{:S(2)}, u32[]{:S(2)}) %all-to-all-start) | async-done | bytes 1966112 | tf_op jit(solution)/shard_map/all_to_all | solution.py:190
  92.5 5.2 %reshape.93 = bf16[1280,8,48,2]{0,3,2,1:T(2,128)(2,1)} reshape(bf16[8,160,768]{1,0,2:T(8,128)(2,1)S(1)} %copy.79) | data formatting | bytes 3932160 | tf_op jit(solution)/shard_map/reshape | solution.py:192
  97.7 10.6 %fusion.14 = bf16[8,48,2560]{2,1,0:T(8,128)(2,1)S(1)} fusion(bf16[2,1280,2560]{2,1,0:T(8,128)(2,1)} %shard_map.128, bf16[1280,8,48,2]{0,3,2,1:T(2,128)(2,1)} %reshape.93), kind=kOutput, calls=%fused_computation.16 | convolution fusion | flops 5034147840 | bytes 17039360 | tf_op jit(solution)/shard_map/glkc,cgn->lkn/dot_general | solution.py:195
  108.3 5.2 %copy.85 = bf16[8,48,2560]{1,0,2:T(8,128)(2,1)} copy(bf16[8,48,2560]{2,1,0:T(8,128)(2,1)S(1)} %fusion.14) | data formatting | bytes 3932160 | tf_op jit(solution)/shard_map/convert_element_type | solution.py:197
  113.5 8.8 %reshape.107 = bf16[4,2,122880]{2,1,0:T(2,128)(2,1)S(1)} reshape(bf16[2560,8,48]{2,1,0:T(8,128)(2,1)} %bitcast.83) | data formatting | bytes 3932160
  122.3 27.7 %all_to_all.83 = bf16[4,2,122880]{2,1,0:T(2,128)(2,1)} all-to-all(bf16[4,2,122880]{2,1,0:T(2,128)(2,1)S(1)} %reshape.107), channel_id=1, replica_groups=mesh['lat'=8,'lon'=4] {'lon'}, dimensions={0} | all-to-all | bytes 3932160 | tf_op jit(solution)/shard_map/all_to_all | solution.py:198
  150.0 7.0 %reshape.108 = bf16[2560,8,48]{2,1,0:T(8,128)(2,1)} reshape(bf16[4,2,122880]{2,1,0:T(2,128)(2,1)} %all_to_all.83) | data formatting | bytes 3932160
  157.1 5.7 %copy.86 = bf16[8,48,4,640]{3,1,2,0:T(8,128)(2,1)S(1)} copy(bf16[8,48,4,640]{1,0,3,2:T(8,128)(2,1)} %bitcast.84) | data formatting | bytes 3932160 | tf_op jit(solution)/shard_map/all_to_all | solution.py:198
  162.9 5.6 %multiply_convert_fusion = (bf16[8,640,512]{2,1,0:T(8,128)(2,1)}, f32[8,640,512]{2,1,0:T(8,128)S(1)}) fusion(f32[512]{0:T(512)S(1)} %copy-done.9, bf16[8,192,640]{2,1,0:T(8,128)(2,1)S(1)} %bitcast.92, bf16[192,512]{1,0:T(8,128)(2,1)S(1)} %copy-done), kind=kOutput, calls=%fused_computation.14 | convolution fusion | flops 1032847360 | bytes 17893376 | tf_op jit(solution)/shard_map/lkc,kh->lch/dot_general | solution.py:200
  168.5 8.7 %convert_reduce_fusion = (f32[512]{0:T(512)S(1)}, bf16[8,640,512]{2,1,0:T(8,128)(2,1)S(1)}) fusion(f32[8,640,512]{2,1,0:T(8,128)S(1)} %get-tuple-element.17, f32[512]{0:T(512)S(1)} %copy-done.9, bf16[8,192,640]{2,1,0:T(8,128)(2,1)S(1)} %copy-done.4, bf16[512,192]{0,1:T(8,128)(2,1)S(1)} %copy-done.8), kind=kOutput, calls=%fused_computation.13 | convolution fusion | flops 1066925568 | bytes 17895424 | tf_op jit(solution)/shard_map/lkc,hk->lch/dot_general | solution.py:212
  189.4 4.4 %convolution_bitcast_fusion.1 = f32[192,512]{1,0:T(8,128)S(1)} fusion(bf16[8,192,640]{2,1,0:T(8,128)(2,1)} %bitcast.93, bf16[8,640,512]{2,1,0:T(8,128)(2,1)} %copy-done.3), kind=kOutput, calls=%fused_computation.29 | convolution fusion | flops 1006632960 | bytes 7602176 | tf_op jit(solution)/shard_map/lkc,lch->kh/dot_general | solution.py:216
  198.2 13.5 %all-to-all-done.2 = bf16[8,192,640]{2,0,1:T(8,128)(2,1)S(1)} async-done(((bf16[8,192,640]{2,0,1:T(8,128)(2,1)}), bf16[8,192,640]{2,0,1:T(8,128)(2,1)S(1)}, u32[]{:S(2)}, u32[]{:S(2)}) %all-to-all-start.2) | async-done | bytes 1966112 | tf_op jit(solution)/shard_map/all_to_all | solution.py:241
  220.6 15.0 %all-to-all-done.4 = f32[32,1,6272]{2,1,0:T(1,128)S(1)} async-done(((f32[32,1,6272]{2,1,0:T(1,128)}), f32[32,1,6272]{2,1,0:T(1,128)S(1)}, u32[]{:S(2)}, u32[]{:S(2)}) %all-to-all-start.4) | async-done | bytes 802848 | tf_op jit(solution)/shard_map/all_to_all | solution.py:78
  241.1 8.6 %fusion.20 = bf16[1280,8,48,2]{0,2,3,1:T(8,128)(2,1)S(1)} fusion(bf16[2,1280,2560]{2,1,0:T(8,128)(2,1)} %shard_map.128, bf16[8,48,2560,1]{2,1,0,3:T(8,128)(2,1)S(1)} %reshape.102), kind=kOutput, calls=%fused_computation.20 | convolution fusion | flops 5034147840 | bytes 17039360 | tf_op jit(solution)/shard_map/cgn,lkn->glkc/dot_general | solution.py:242
  252.4 6.4 %all_to_all.71 = bf16[8,160,768]{1,0,2:T(8,128)(2,1)S(1)} reshape(bf16[1280,8,48,2]{0,3,2,1:T(2,128)(2,1)} %copy.89) | data formatting | bytes 3932160 | tf_op jit(solution)/shard_map/all_to_all | solution.py:246
  262.1 6.0 %all-to-all-start.3 = ((bf16[8,160,768]{2,1,0:T(8,128)(2,1)}), bf16[8,160,768]{2,1,0:T(8,128)(2,1)S(1)}, u32[]{:S(2)}, u32[]{:S(2)}) async-start(bf16[8,160,768]{2,1,0:T(8,128)(2,1)} %copy.90), calls=%async_computation.3 | async-start | bytes 3932160 | tf_op jit(solution)/shard_map/all_to_all | solution.py:246
  268.2 5.6 %fusion.25 = bf16[8,192,640]{2,1,0:T(8,128)(2,1)} fusion(f32[192]{0:T(256)S(1)} %copy-done.10, bf16[8,640,512]{2,1,0:T(8,128)(2,1)} %get-tuple-element.16, bf16[512,192]{0,1:T(8,128)(2,1)S(1)} %copy-done.8), kind=kOutput, calls=%fused_computation.27 | convolution fusion | flops 1008599040 | bytes 7406336 | tf_op jit(solution)/shard_map/lch,hk->lkc/dot_general | solution.py:205
  282.5 31.4 %all-to-all-done.3 = bf16[8,160,768]{2,1,0:T(8,128)(2,1)S(1)} async-done(((bf16[8,160,768]{2,1,0:T(8,128)(2,1)}), bf16[8,160,768]{2,1,0:T(8,128)(2,1)S(1)}, u32[]{:S(2)}, u32[]{:S(2)}) %all-to-all-start.3) | async-done | bytes 1966112 | tf_op jit(solution)/shard_map/all_to_all | solution.py:246
  316.2 4.6 %reshape.94 = bf16[80,2,64,96]{3,2,1,0:T(8,128)(2,1)S(1)} reshape(bf16[160,8,768]{2,1,0:T(8,128)(2,1)} %copy.91) | data formatting | bytes 3932160 | tf_op jit(solution)/shard_map/reshape | solution.py:247
  323.2 4.7 %rev.8 = bf16[80,2,32,96]{3,2,1,0:T(8,128)(2,1)} reverse(bf16[80,2,32,96]{3,2,1,0:T(8,128)(2,1)} %get-tuple-element.7), dimensions={2} | reverse | bytes 1966080 | tf_op jit(solution)/shard_map/jit(_flip)/rev | solution.py:249
  333.5 16.9 %shard_map.129 = bf16[80,96,1408]{2,1,0:T(8,128)(2,1)} custom-call(s32[80]{0:T(128)} %dynamic_slice.3.ids_ref, bf16[80,96,128]{2,1,0:T(8,128)(2,1)} %bitcast.90, bf16[80,32,1408]{2,1,0:T(8,128)(2,1)} %basis_ref.3), custom_call_target="tpu_custom_call" | custom-call | tf_op jit(solution)/shard_map/pallas_call | solution.py:164
  (74 shorter events, 86.7 us)
Async XLA Ops:
  0.6 162.2 %copy-start = (bf16[192,512]{1,0:T(8,128)(2,1)S(1)}, bf16[192,512]{1,0:T(8,128)(2,1)}, u32[]{:S(2)}) copy-start(bf16[192,512]{1,0:T(8,128)(2,1)} %param.11) | copy-start | bytes 589828
  27.6 14.2 %copy-start.7 = (s32[640]{0:T(1024)S(1)}, s32[640]{0:T(1024)}, u32[]{:S(2)}) copy-start(s32[640]{0:T(1024)} %param.8) | copy-start | bytes 7684
  33.9 53.2 %all-to-all-start = ((bf16[160,8,768]{2,0,1:T(8,128)(2,1)}), bf16[160,8,768]{2,0,1:T(8,128)(2,1)S(1)}, u32[]{:S(2)}, u32[]{:S(2)}) async-start(bf16[160,8,768]{2,0,1:T(8,128)(2,1)} %copy.78), calls=%async_computation | async-start | bytes 3932160 | tf_op jit(solution)/shard_map/all_to_all | solution.py:190
  87.1 1.3 copy-start.2
  157.1 5.8 %copy-start.9 = (f32[512]{0:T(512)S(1)}, f32[512]{0:T(512)}, u32[]{:S(2)}) copy-start(f32[512]{0:T(512)} %param.12) | copy-start | bytes 6148
  162.8 5.6 %copy-start.6 = (bf16[8,48,4,640]{3,1,2,0:T(8,128)(2,1)}, bf16[8,48,4,640]{3,1,2,0:T(8,128)(2,1)S(1)}, u32[]{:S(2)}) copy-start(bf16[8,48,4,640]{3,1,2,0:T(8,128)(2,1)S(1)} %copy.86) | copy-start | bytes 5898244
  162.9 5.6 %copy-start.4 = (bf16[8,192,640]{2,1,0:T(8,128)(2,1)S(1)}, bf16[8,192,640]{2,1,0:T(8,128)(2,1)}, u32[]{:S(2)}) copy-start(bf16[8,192,640]{2,1,0:T(8,128)(2,1)} %param.15) | copy-start | bytes 5898244
  162.9 5.6 %copy-start.8 = (bf16[512,192]{0,1:T(8,128)(2,1)S(1)}, bf16[512,192]{0,1:T(8,128)(2,1)}, u32[]{:S(2)}) copy-start(bf16[512,192]{0,1:T(8,128)(2,1)} %param.13) | copy-start | bytes 589828
  177.2 2.4 copy-start.3
  183.8 27.9 %all-to-all-start.2 = ((bf16[8,192,640]{2,0,1:T(8,128)(2,1)}), bf16[8,192,640]{2,0,1:T(8,128)(2,1)S(1)}, u32[]{:S(2)}, u32[]{:S(2)}) async-start(bf16[8,192,640]{2,0,1:T(8,128)(2,1)} %copy.87), calls=%async_computation.2 | async-start | bytes 3932160 | tf_op jit(solution)/shard_map/all_to_all | solution.py:241
  187.4 6.5 %slice-start = ((s8[5242880]{0:T(1024)(128)(4,1)}), s8[4194304]{0:T(1024)(128)(4,1)S(1)}, s32[]{:S(2)}) async-start(s8[5242880]{0:T(1024)(128)(4,1)} %bitcast.97), calls=%async_computation.6 | async-start | bytes 8388608
  189.4 4.4 %copy-start.5 = (bf16[8,192,640]{2,1,0:T(8,128)(2,1)S(1)}, bf16[8,192,640]{2,1,0:T(8,128)(2,1)}, u32[]{:S(2)}) copy-start(bf16[8,192,640]{2,1,0:T(8,128)(2,1)} %param.15) | copy-start | bytes 5898244
  189.4 4.4 %slice-start.1 = ((s8[5242880]{0:T(1024)(128)(4,1)}), s8[1048576]{0:T(1024)(128)(4,1)S(1)}, s32[]{:S(2)}) async-start(s8[5242880]{0:T(1024)(128)(4,1)} %bitcast.97), calls=%async_computation.7 | async-start | bytes 2097152
  211.6 23.9 %all-to-all-start.4 = ((f32[32,1,6272]{2,1,0:T(1,128)}), f32[32,1,6272]{2,1,0:T(1,128)S(1)}, u32[]{:S(2)}, u32[]{:S(2)}) async-start(f32[32,1,6272]{2,1,0:T(1,128)} %bitcast.25), calls=%async_computation.4 | async-start | bytes 1605632 | tf_op jit(solution)/shard_map/all_to_all | solution.py:78
  237.3 24.8 %all-to-all-start.5 = ((f32[32,1,6272]{2,1,0:T(1,128)}), f32[32,1,6272]{2,1,0:T(1,128)}, u32[]{:S(2)}, u32[]{:S(2)}) async-start(f32[32,1,6272]{2,1,0:T(1,128)} %broadcast_in_dim.29), calls=%async_computation.5 | async-start | bytes 1605632 | tf_op jit(solution)/shard_map/all_to_all | solution.py:81
  258.9 9.3 %copy-start.10 = (f32[192]{0:T(256)S(1)}, f32[192]{0:T(256)}, u32[]{:S(2)}) copy-start(f32[192]{0:T(256)} %param.14) | copy-start | bytes 2308
  262.1 51.7 %all-to-all-start.3 = ((bf16[8,160,768]{2,1,0:T(8,128)(2,1)}), bf16[8,160,768]{2,1,0:T(8,128)(2,1)S(1)}, u32[]{:S(2)}, u32[]{:S(2)}) async-start(bf16[8,160,768]{2,1,0:T(8,128)(2,1)} %copy.90), calls=%async_computation.3 | async-start | bytes 3932160 | tf_op jit(solution)/shard_map/all_to_all | solution.py:246
  333.5 16.9 %copy-start.1 = (bf16[192,512]{1,0:T(8,128)(2,1)S(1)}, bf16[192,512]{1,0:T(8,128)(2,1)}, u32[]{:S(2)}) copy-start(bf16[192,512]{1,0:T(8,128)(2,1)} %param.11) | copy-start | bytes 589828
where the time goes:
time: 356 us; the launch traced here: 351 us
  local copies, waits for them, and re-layouts  103 us (29%)
  waiting for transfers between devices  83.2 us (23%)
  Pallas kernels  46.7 us (13%)
  matrix products  46.4 us (13%)
  blocking collectives  27.7 us (8%)
  starting transfers between devices  24.2 us (7%)
  other arithmetic  18 us (5%)
    all_to_all x1, waiting for transfers between devices, per_device(): lax.all_to_all(flat_grad, 'lat', split_axis=0, concat_axis=1, tiled=True)  31.4 us
    all_to_all x1, blocking collectives, per_device(): lax.all_to_all(all_columns, 'lon', split_axis=2, concat_axis=1, tiled=True)  27.7 us
    all_to_all x1, waiting for transfers between devices, per_device(): lax.all_to_all(flat_waves, 'lat', split_axis=1, concat_axis=0, tiled=True)  23.4 us
    unnamed x28, local copies, waits for them, and re-layouts  19.6 us
    pallas_call x1, Pallas kernels, synthesis(): pl.pallas_call(synth_kernel, grid_spec=spec, out_shape=jax.ShapeDtypeStru...  17.1 us
    pallas_call x1, Pallas kernels, analysis(): pl.pallas_call(analyse_kernel, grid_spec=spec, out_shape=jax.ShapeDtypeSt...  16.9 us
    all_to_all x1, waiting for transfers between devices, all_reduce(): parts = lax.all_to_all(flat.reshape(count, chunk), axes, 0, 0, tiled=True)  15 us
    all_to_all x1, waiting for transfers between devices, per_device(): lax.all_to_all(grid_grad, 'lon', split_axis=1, concat_axis=2, tiled=True)  13.5 us
  transfers between devices with their start and end apart: 5, of which 4 were waited for; matrix products, arithmetic and copies ran while one was open for 16% of the time, Pallas kernels for 4%

commit v1 on v0

--- a/solution.py
+++ b/solution.py
@@ -192,10 +192,13 @@
     coeff_grid = band_waves.reshape(wave_count, band_rows, width_local // 2, 2)
     numbers = wave_numbers(pair_table)
     full_table = fourier_table(numbers, lon_total)
+    lon_parts = lax.axis_size("lon")
+    block_table = full_table.reshape(2, wave_count, lon_parts, block_cols)
     all_columns = jnp.einsum(
-        "glkc,cgn->lkn", coeff_grid, full_table, preferred_element_type=jnp.float32
-    ).astype(jnp.bfloat16)
-    grid = lax.all_to_all(all_columns, "lon", split_axis=2, concat_axis=1, tiled=True)
+        "glkc,cgbn->blkn", coeff_grid, block_table, preferred_element_type=jnp.float32
+    ).astype(jnp.bfloat16)
+    level_blocks = lax.all_to_all(all_columns, "lon", 0, 0, tiled=True)
+    grid = jnp.swapaxes(level_blocks, 0, 1).reshape(band_rows, -1, block_cols)
     pre_act = (
         jnp.einsum("lkc,kh->lch", grid, in_weight, preferred_element_type=jnp.float32) + in_bias
     )
@@ -238,9 +241,10 @@
     out_weight_grad = summed[channels : 2 * channels, :hid].T
     in_bias_grad = summed[2 * channels, :hid]
     out_bias_grad = summed[2 * channels + 1, :channels]
-    level_rows = lax.all_to_all(grid_grad, "lon", split_axis=1, concat_axis=2, tiled=True)
+    grad_blocks = jnp.swapaxes(grid_grad.reshape(band_rows, lon_parts, -1, block_cols), 0, 1)
+    level_rows = lax.all_to_all(grad_blocks, "lon", 0, 0, tiled=True)
     wave_grad = jnp.einsum(
-        "cgn,lkn->glkc", full_table, level_rows, preferred_element_type=jnp.float32
+        "cgbn,blkn->glkc", block_table, level_rows, preferred_element_type=jnp.float32
     ).astype(jnp.bfloat16)
     flat_grad = wave_grad.reshape(wave_count, band_rows * width_local)
     pair_grad = lax.all_to_all(flat_grad, "lat", split_axis=0, concat_axis=1, tiled=True)

time: 356 us -> 329 us (0.924)
  blocking collectives: 27.7 us -> 0 us
  local copies, waits for them, and re-layouts: 103 us -> 89.4 us
  waiting for transfers between devices: 83.2 us -> 93.2 us
  starting transfers between devices: 24.2 us -> 29.7 us
    all_to_all x1 -> x2, waiting for transfers between devices: 13.5 us -> 46.1 us  [the longest x1 23.8 us: per_device(): level_rows = lax.all_to_all(grad_blocks, 'lon', 0, 0, tiled=True)]
    all_to_all x1 -> x0, blocking collectives: 27.7 us -> none  [per_device(): lax.all_to_all(all_columns, 'lon', split_axis=2, concat_axis=1, tiled=True)]
    reshape x0 -> x2, local copies, waits for them, and re-layouts: none -> 24.4 us  [the longest x1 23 us: per_device(): block_table = full_table.reshape(2, wave_count, lon_parts, block_cols)]
    all_to_all x1, waiting for transfers between devices: 23.4 us -> 0.4 us  [per_device(): lax.all_to_all(flat_waves, 'lat', split_axis=1, concat_axis=0, tiled=True)]
    unnamed x28 -> x18, local copies, waits for them, and re-layouts: 19.6 us -> 2.46 us
    all_to_all x3 -> x0, local copies, waits for them, and re-layouts: 11.7 us -> none  [the longest x2 5.96 us: per_device(): lax.all_to_all(grid_grad, 'lon', split_axis=1, concat_axis=2, tiled=True)]
    convert_element_type x3 -> x1, local copies, waits for them, and re-layouts: 10.4 us -> 2.79 us  [per_device(): wave_grad = jnp.einsum('cgbn,blkn->glkc', block_table, level_rows, prefer...]
    all_to_all x1 -> x2, starting transfers between devices: 3.6 us -> 7.5 us  [the longest x1 3.9 us: per_device(): level_blocks = lax.all_to_all(all_columns, 'lon', 0, 0, tiled=True)]
  transfers between devices with their start and end apart: 5 -> 6, of which waited for: 4 -> 6; matrix products, arithmetic and copies ran while one was open for 16% -> 21% of each run, Pallas kernels for 4% -> 4%
where the time goes in v1:
time: 329 us; the launch traced here: 323 us
  waiting for transfers between devices  93.2 us (28%)
  local copies, waits for them, and re-layouts  89.4 us (27%)
  Pallas kernels  46.6 us (14%)
  matrix products  45 us (14%)
  starting transfers between devices  29.7 us (9%)
  other arithmetic  17.8 us (5%)
    all_to_all x1, waiting for transfers between devices, per_device(): lax.all_to_all(flat_grad, 'lat', split_axis=0, concat_axis=1, tiled=True)  31.4 us
    all_to_all x1, waiting for transfers between devices, per_device(): level_rows = lax.all_to_all(grad_blocks, 'lon', 0, 0, tiled=True)  23.8 us
    reshape x1, local copies, waits for them, and re-layouts, per_device(): block_table = full_table.reshape(2, wave_count, lon_parts, block_cols)  23 us
    all_to_all x1, waiting for transfers between devices, per_device(): level_blocks = lax.all_to_all(all_columns, 'lon', 0, 0, tiled=True)  22.3 us
    pallas_call x1, Pallas kernels, synthesis(): pl.pallas_call(synth_kernel, grid_spec=spec, out_shape=jax.ShapeDtypeStru...  17.1 us
    pallas_call x1, Pallas kernels, analysis(): pl.pallas_call(analyse_kernel, grid_spec=spec, out_shape=jax.ShapeDtypeSt...  16.7 us
    all_to_all x1, waiting for transfers between devices, all_reduce(): parts = lax.all_to_all(flat.reshape(count, chunk), axes, 0, 0, tiled=True)  15.2 us
    pallas_call x1, Pallas kernels, fourier_table(): pl.pallas_call(table_kernel, grid=(count // rows,), in_specs=[pl.BlockSpe...  12.7 us
  transfers between devices with their start and end apart: 6, of which 6 were waited for; matrix products, arithmetic and copies ran while one was open for 21% of the time, Pallas kernels for 4%

profile of v1, /device:TPU:0, one launch (start us, length us, event | category | flops | bytes accessed | tf_op | source)
XLA Modules:
  0.0 322.9 jit_solution(3208458205759482563)
XLA Ops:
  2.0 17.1 %shard_map.128 = bf16[80,128,96]{2,1,0:T(8,128)(2,1)} custom-call(s32[80]{0:T(128)} %dynamic_slice.3.ids_ref, bf16[80,96,1408]{2,1,0:T(8,128)(2,1)} %spec_ref.1, bf16[80,32,1408]{2,1,0:T(8,128)(2,1)} %basis_ref.3), custom_call_target="tpu_custom_call" | custom-call | tf_op jit(solution)/shard_map/pallas_call | solution.py:143
  33.9 7.8 %all-to-all-start = ((bf16[160,8,768]{2,0,1:T(8,128)(2,1)}), bf16[160,8,768]{2,0,1:T(8,128)(2,1)S(1)}, u32[]{:S(2)}, u32[]{:S(2)}) async-start(bf16[160,8,768]{2,0,1:T(8,128)(2,1)} %copy.87), calls=%async_computation | async-start | bytes 3932160 | tf_op jit(solution)/shard_map/all_to_all | solution.py:190
  43.8 4.0 %fusion.27 = (f32[1280,128]{1,0:T(8,128)}, f32[1280,128]{1,0:T(8,128)}) fusion(s32[1280]{0:T(1024)S(1)} %mul.94), kind=kLoop, calls=%fused_computation.40 | loop fusion | flops 1474560 | bytes 1315840 | tf_op jit(solution)/shard_map/sin | solution.py:50
  51.0 12.7 %shard_map.127 = bf16[2,1280,2560]{2,1,0:T(8,128)(2,1)} custom-call(f32[1280,20]{1,0:T(8,128)} %get-tuple-element.13.cos_a_ref, f32[1280,20]{1,0:T(8,128)} %get-tuple-element.12.sin_a_ref, f32[1280,128]{1,0:T(8,128)} %get-tuple-element.15.cos_b_ref, f32[1280,128]{1,0:T(8,128)} %get-tuple-element.14.sin_b_ref, f32[1280,1]{1,0:T(8,128)} %select_n.35.factor_ref), custom_call_target="tpu_custom_call" | custom-call | tf_op jit(solution)/shard_map/pallas_call | solution.py:56
  63.7 23.0 %reshape.101 = bf16[2,1280,4,640]{3,2,1,0:T(4,128)(2,1)} reshape(bf16[2,1280,2560]{2,1,0:T(8,128)(2,1)} %shard_map.127) | data formatting | bytes 26214400 | tf_op jit(solution)/shard_map/reshape | solution.py:196
  88.4 4.1 %copy.88 = bf16[8,160,768]{1,0,2:T(8,128)(2,1)S(1)} copy(bf16[8,160,768]{2,1,0:T(8,128)(2,1)} %bitcast.100) | data formatting | bytes 3932160 | tf_op jit(solution)/shard_map/all_to_all | solution.py:190
  92.5 5.2 %reshape.103 = bf16[1280,8,48,2]{0,3,2,1:T(2,128)(2,1)} reshape(bf16[8,160,768]{1,0,2:T(8,128)(2,1)S(1)} %copy.88) | data formatting | bytes 3932160 | tf_op jit(solution)/shard_map/reshape | solution.py:192
  97.7 11.8 %fusion.18 = bf16[4,8,48,640]{3,2,1,0:T(8,128)(2,1)} fusion(bf16[1280,8,48,2]{0,3,2,1:T(2,128)(2,1)} %reshape.103, bf16[2,1280,4,640,1]{3,2,1,0,4:T(4,128)(2,1)} %bitcast.96), kind=kOutput, calls=%fused_computation.29 | convolution fusion | flops 5034147840 | bytes 17039360 | tf_op jit(solution)/shard_map/glkc,cgbn->blkn/dot_general | solution.py:197
  109.5 3.9 %all-to-all-start.1 = ((bf16[4,8,48,640]{3,2,1,0:T(8,128)(2,1)}), bf16[4,8,48,640]{3,2,1,0:T(8,128)(2,1)S(1)}, u32[]{:S(2)}, u32[]{:S(2)}) async-start(bf16[4,8,48,640]{3,2,1,0:T(8,128)(2,1)} %fusion.18), calls=%async_computation.1 | async-start | bytes 3932160 | tf_op jit(solution)/shard_map/all_to_all | solution.py:200
  115.3 22.3 %all-to-all-done.1 = bf16[4,8,48,640]{3,2,1,0:T(8,128)(2,1)S(1)} async-done(((bf16[4,8,48,640]{3,2,1,0:T(8,128)(2,1)}), bf16[4,8,48,640]{3,2,1,0:T(8,128)(2,1)S(1)}, u32[]{:S(2)}, u32[]{:S(2)}) %all-to-all-start.1) | async-done | bytes 1966112 | tf_op jit(solution)/shard_map/all_to_all | solution.py:200
  137.9 3.8 %multiply_convert_fusion = (bf16[8,640,512]{2,1,0:T(8,128)(2,1)S(1)}, f32[8,640,512]{2,1,0:T(8,128)S(1)}) fusion(f32[512]{0:T(512)S(1)} %copy-done.6, bf16[8,192,640]{2,1,0:T(8,128)(2,1)S(1)} %bitcast.104, bf16[192,512]{1,0:T(8,128)(2,1)S(1)} %copy-done), kind=kOutput, calls=%fused_computation.15 | convolution fusion | flops 1032847360 | bytes 17893376 | tf_op jit(solution)/shard_map/lkc,kh->lch/dot_general | solution.py:203
  141.8 8.7 %convert_reduce_fusion = (f32[512]{0:T(512)S(1)}, bf16[8,640,512]{2,1,0:T(8,128)(2,1)S(1)}) fusion(f32[8,640,512]{2,1,0:T(8,128)S(1)} %get-tuple-element.17, f32[512]{0:T(512)S(1)} %copy-done.6, bf16[8,192,640]{2,1,0:T(8,128)(2,1)S(1)} %copy-done.3, bf16[512,192]{0,1:T(8,128)(2,1)S(1)} %copy-done.5), kind=kOutput, calls=%fused_computation.14 | convolution fusion | flops 1066925568 | bytes 17895424 | tf_op jit(solution)/shard_map/lkc,hk->lch/dot_general | solution.py:215
  155.1 4.7 %all-to-all-start.4 = ((f32[32,1,6272]{2,1,0:T(1,128)}), f32[32,1,6272]{2,1,0:T(1,128)S(1)}, u32[]{:S(2)}, u32[]{:S(2)}) async-start(f32[32,1,6272]{2,1,0:T(1,128)} %bitcast.28), calls=%async_computation.4 | async-start | bytes 1605632 | tf_op jit(solution)/shard_map/all_to_all | solution.py:78
  159.8 4.3 %convolution_convert_fusion = bf16[8,640,192]{1,2,0:T(8,128)(2,1)S(1)} fusion(bf16[8,640,512]{2,1,0:T(8,128)(2,1)} %copy-done.2, bf16[192,512]{1,0:T(8,128)(2,1)S(1)} %copy-done), kind=kOutput, calls=%fused_computation.27 | convolution fusion | flops 1007616000 | bytes 7405568 | tf_op jit(solution)/shard_map/lch,kh->lkc/dot_general | solution.py:221
  165.5 15.2 %all-to-all-done.4 = f32[32,1,6272]{2,1,0:T(1,128)S(1)} async-done(((f32[32,1,6272]{2,1,0:T(1,128)}), f32[32,1,6272]{2,1,0:T(1,128)S(1)}, u32[]{:S(2)}, u32[]{:S(2)}) %all-to-all-start.4) | async-done | bytes 802848 | tf_op jit(solution)/shard_map/all_to_all | solution.py:78
  184.8 23.8 %all-to-all-done.2 = bf16[4,8,48,640]{3,2,1,0:T(8,128)(2,1)S(1)} async-done(((bf16[4,8,48,640]{3,2,1,0:T(8,128)(2,1)}), bf16[4,8,48,640]{3,2,1,0:T(8,128)(2,1)S(1)}, u32[]{:S(2)}, u32[]{:S(2)}) %all-to-all-start.2) | async-done | bytes 1966112 | tf_op jit(solution)/shard_map/all_to_all | solution.py:245
  213.5 8.4 %fusion.11 = bf16[1280,8,48,2]{0,2,3,1:T(8,128)(2,1)S(1)} fusion(bf16[2,160,4,8,640]{4,3,2,1,0:T(8,128)(2,1)} %bitcast.95, bf16[4,8,48,640]{3,2,1,0:T(8,128)(2,1)S(1)} %all-to-all-done.2), kind=kOutput, calls=%fused_computation.20 | convolution fusion | flops 5034147840 | bytes 17039360 | tf_op jit(solution)/shard_map/cgbn,blkn->glkc/dot_general | solution.py:246
  224.6 6.4 %all_to_all.45 = bf16[8,160,768]{1,0,2:T(8,128)(2,1)S(1)} reshape(bf16[1280,8,48,2]{0,3,2,1:T(2,128)(2,1)} %copy.95) | data formatting | bytes 3932160 | tf_op jit(solution)/shard_map/all_to_all | solution.py:250
  234.4 6.1 %all-to-all-start.3 = ((bf16[8,160,768]{2,1,0:T(8,128)(2,1)}), bf16[8,160,768]{2,1,0:T(8,128)(2,1)S(1)}, u32[]{:S(2)}, u32[]{:S(2)}) async-start(bf16[8,160,768]{2,1,0:T(8,128)(2,1)} %copy.96), calls=%async_computation.3 | async-start | bytes 3932160 | tf_op jit(solution)/shard_map/all_to_all | solution.py:250
  240.6 5.6 %fusion.17 = bf16[8,192,640]{2,1,0:T(8,128)(2,1)} fusion(f32[192]{0:T(256)S(1)} %copy-done.7, bf16[8,640,512]{2,1,0:T(8,128)(2,1)} %copy-done.8, bf16[512,192]{0,1:T(8,128)(2,1)S(1)} %copy-done.5), kind=kOutput, calls=%fused_computation.28 | convolution fusion | flops 1008599040 | bytes 7406336 | tf_op jit(solution)/shard_map/lch,hk->lkc/dot_general | solution.py:208
  254.9 31.4 %all-to-all-done.3 = bf16[8,160,768]{2,1,0:T(8,128)(2,1)S(1)} async-done(((bf16[8,160,768]{2,1,0:T(8,128)(2,1)}), bf16[8,160,768]{2,1,0:T(8,128)(2,1)S(1)}, u32[]{:S(2)}, u32[]{:S(2)}) %all-to-all-start.3) | async-done | bytes 1966112 | tf_op jit(solution)/shard_map/all_to_all | solution.py:250
  288.6 4.6 %reshape.106 = bf16[80,2,64,96]{3,2,1,0:T(8,128)(2,1)S(1)} reshape(bf16[160,8,768]{2,1,0:T(8,128)(2,1)} %copy.97) | data formatting | bytes 3932160 | tf_op jit(solution)/shard_map/reshape | solution.py:251
  295.5 4.7 %rev.8 = bf16[80,2,32,96]{3,2,1,0:T(8,128)(2,1)} reverse(bf16[80,2,32,96]{3,2,1,0:T(8,128)(2,1)} %get-tuple-element.7), dimensions={2} | reverse | bytes 1966080 | tf_op jit(solution)/shard_map/jit(_flip)/rev | solution.py:253
  305.9 16.7 %shard_map.129 = bf16[80,96,1408]{2,1,0:T(8,128)(2,1)} custom-call(s32[80]{0:T(128)} %dynamic_slice.3.ids_ref, bf16[80,96,128]{2,1,0:T(8,128)(2,1)} %bitcast.103, bf16[80,32,1408]{2,1,0:T(8,128)(2,1)} %basis_ref.3), custom_call_target="tpu_custom_call" | custom-call | tf_op jit(solution)/shard_map/pallas_call | solution.py:164
  (62 shorter events, 65.3 us)
Async XLA Ops:
  0.6 137.3 %copy-start = (bf16[192,512]{1,0:T(8,128)(2,1)S(1)}, bf16[192,512]{1,0:T(8,128)(2,1)}, u32[]{:S(2)}) copy-start(bf16[192,512]{1,0:T(8,128)(2,1)} %param.11) | copy-start | bytes 589828
  27.6 14.2 %copy-start.4 = (s32[640]{0:T(1024)S(1)}, s32[640]{0:T(1024)}, u32[]{:S(2)}) copy-start(s32[640]{0:T(1024)} %param.8) | copy-start | bytes 7684
  33.9 53.2 %all-to-all-start = ((bf16[160,8,768]{2,0,1:T(8,128)(2,1)}), bf16[160,8,768]{2,0,1:T(8,128)(2,1)S(1)}, u32[]{:S(2)}, u32[]{:S(2)}) async-start(bf16[160,8,768]{2,0,1:T(8,128)(2,1)} %copy.87), calls=%async_computation | async-start | bytes 3932160 | tf_op jit(solution)/shard_map/all_to_all | solution.py:190
  87.1 1.3 copy-start.1
  109.5 28.4 %copy-start.6 = (f32[512]{0:T(512)S(1)}, f32[512]{0:T(512)}, u32[]{:S(2)}) copy-start(f32[512]{0:T(512)} %param.12) | copy-start | bytes 6148
  109.5 28.2 %all-to-all-start.1 = ((bf16[4,8,48,640]{3,2,1,0:T(8,128)(2,1)}), bf16[4,8,48,640]{3,2,1,0:T(8,128)(2,1)S(1)}, u32[]{:S(2)}, u32[]{:S(2)}) async-start(bf16[4,8,48,640]{3,2,1,0:T(8,128)(2,1)} %fusion.18), calls=%async_computation.1 | async-start | bytes 3932160 | tf_op jit(solution)/shard_map/all_to_all | solution.py:200
  137.9 3.8 %copy-start.3 = (bf16[8,192,640]{2,1,0:T(8,128)(2,1)S(1)}, bf16[8,192,640]{2,1,0:T(8,128)(2,1)}, u32[]{:S(2)}) copy-start(bf16[8,192,640]{2,1,0:T(8,128)(2,1)} %param.15) | copy-start | bytes 5898244
  137.9 3.8 %copy-start.5 = (bf16[512,192]{0,1:T(8,128)(2,1)S(1)}, bf16[512,192]{0,1:T(8,128)(2,1)}, u32[]{:S(2)}) copy-start(bf16[512,192]{0,1:T(8,128)(2,1)} %param.13) | copy-start | bytes 589828
  141.7 11.1 %copy-start.8 = (bf16[8,640,512]{2,1,0:T(8,128)(2,1)}, bf16[8,640,512]{2,1,0:T(8,128)(2,1)S(1)}, u32[]{:S(2)}) copy-start(bf16[8,640,512]{2,1,0:T(8,128)(2,1)S(1)} %get-tuple-element.16) | copy-start | bytes 15728644
  150.5 2.3 copy-start.2
  155.1 25.7 %all-to-all-start.4 = ((f32[32,1,6272]{2,1,0:T(1,128)}), f32[32,1,6272]{2,1,0:T(1,128)S(1)}, u32[]{:S(2)}, u32[]{:S(2)}) async-start(f32[32,1,6272]{2,1,0:T(1,128)} %bitcast.28), calls=%async_computation.4 | async-start | bytes 1605632 | tf_op jit(solution)/shard_map/all_to_all | solution.py:78
  180.7 27.9 %all-to-all-start.2 = ((bf16[4,8,48,640]{3,2,1,0:T(8,128)(2,1)}), bf16[4,8,48,640]{3,2,1,0:T(8,128)(2,1)S(1)}, u32[]{:S(2)}, u32[]{:S(2)}) async-start(bf16[4,8,48,640]{3,2,1,0:T(8,128)(2,1)} %bitcast.94), calls=%async_computation.2 | async-start | bytes 3932160 | tf_op jit(solution)/shard_map/all_to_all | solution.py:245
  209.9 24.5 %all-to-all-start.5 = ((f32[32,1,6272]{2,1,0:T(1,128)}), f32[32,1,6272]{2,1,0:T(1,128)}, u32[]{:S(2)}, u32[]{:S(2)}) async-start(f32[32,1,6272]{2,1,0:T(1,128)} %broadcast_in_dim.29), calls=%async_computation.5 | async-start | bytes 1605632 | tf_op jit(solution)/shard_map/all_to_all | solution.py:81
  231.1 9.5 %copy-start.7 = (f32[192]{0:T(256)S(1)}, f32[192]{0:T(256)}, u32[]{:S(2)}) copy-start(f32[192]{0:T(256)} %param.14) | copy-start | bytes 2308
  234.4 51.9 %all-to-all-start.3 = ((bf16[8,160,768]{2,1,0:T(8,128)(2,1)}), bf16[8,160,768]{2,1,0:T(8,128)(2,1)S(1)}, u32[]{:S(2)}, u32[]{:S(2)}) async-start(bf16[8,160,768]{2,1,0:T(8,128)(2,1)} %copy.96), calls=%async_computation.3 | async-start | bytes 3932160 | tf_op jit(solution)/shard_map/all_to_all | solution.py:250

commit v2 on v1

--- a/solution.py
+++ b/solution.py
@@ -121,7 +121,7 @@
 
 
 def pair_block(count):
-    for size in (8, 4, 2, 1):
+    for size in (16, 8, 4, 2, 1):
         if count % size == 0:
             return size
 
@@ -183,9 +183,12 @@
     raw_waves = synthesis(local_ids, spectral, lat_basis).reshape(
         pair_dev, 2, lat_window, width_local
     )
-    waves = jnp.concatenate(
-        [raw_waves[:, :, :lat_half], jnp.flip(raw_waves[:, :, lat_half:], axis=2)], axis=2
-    )
+    lat_index = jnp.arange(lat_window, dtype=jnp.int32)
+    kernel_row = jnp.where(lat_index < lat_half, lat_index, 3 * lat_half - 1 - lat_index)
+    reorder = (kernel_row[:, None] == lat_index[None, :]).astype(jnp.bfloat16)
+    waves = jnp.einsum(
+        "lr,pqrk->pqlk", reorder, raw_waves, preferred_element_type=jnp.float32
+    ).astype(jnp.bfloat16)
     flat_waves = waves.reshape(2 * pair_dev, lat_window * width_local)
     band_waves = lax.all_to_all(flat_waves, "lat", split_axis=1, concat_axis=0, tiled=True)
     wave_count = band_waves.shape[0]
@@ -249,10 +252,9 @@
     flat_grad = wave_grad.reshape(wave_count, band_rows * width_local)
     pair_grad = lax.all_to_all(flat_grad, "lat", split_axis=0, concat_axis=1, tiled=True)
     pair_grad = pair_grad.reshape(pair_dev, 2, lat_window, width_local)
-    pair_grad = jnp.concatenate(
-        [pair_grad[:, :, :lat_half], jnp.flip(pair_grad[:, :, lat_half:], axis=2)], axis=2
-    )
-    pair_grad = jnp.swapaxes(pair_grad.reshape(pair_dev, 2 * lat_window, width_local), 1, 2)
+    pair_grad = jnp.einsum(
+        "lr,pqlk->pkqr", reorder, pair_grad, preferred_element_type=jnp.float32
+    ).astype(jnp.bfloat16).reshape(pair_dev, width_local, 2 * lat_window)
     spectral_grad = analysis(local_ids, pair_grad, lat_basis)
     return (tendency, spectral_grad, in_weight_grad, in_bias_grad, out_weight_grad, out_bias_grad)
 

time: 329 us -> 313 us (0.951)
  local copies, waits for them, and re-layouts: 89.4 us -> 77.6 us
  other arithmetic: 17.8 us -> 12.8 us
  matrix products: 45 us -> 49.9 us
  Pallas kernels: 46.6 us -> 42.8 us
    rev x2 -> x0, local copies, waits for them, and re-layouts: 7.24 us -> none  [the longest x1 4.66 us: per_device(): jnp.flip(pair_grad[:, :, lat_half:], axis=2)]
    slice x2 -> x0, local copies, waits for them, and re-layouts: 5.72 us -> none  [the longest x1 3.35 us: per_device(): raw_waves[:, :, :lat_half]]
    concatenate x2 -> x0, other arithmetic: 5.03 us -> none  [the longest x1 2.52 us: per_device(): jnp.concatenate([raw_waves[:, :, :lat_half], jnp.flip(raw_waves[:, :, lat...]
    dot_general x0 -> x2, matrix products: none -> 4.94 us  [the longest x1 2.63 us: per_device(): jnp.einsum('lr,pqrk->pqlk', reorder, raw_waves, preferred_element_type=jn...]
  transfers between devices with their start and end apart: 6 -> 6, of which waited for: 6 -> 6; matrix products, arithmetic and copies ran while one was open for 21% -> 22% of each run, Pallas kernels for 4% -> 4%
where the time goes in v2:
time: 313 us; the launch traced here: 307 us
  waiting for transfers between devices  93.1 us (30%)
  local copies, waits for them, and re-layouts  77.6 us (25%)
  matrix products  49.9 us (16%)
  Pallas kernels  42.8 us (14%)
  starting transfers between devices  29.8 us (10%)
  other arithmetic  12.8 us (4%)
    all_to_all x1, waiting for transfers between devices, per_device(): lax.all_to_all(flat_grad, 'lat', split_axis=0, concat_axis=1, tiled=True)  31.3 us
    all_to_all x1, waiting for transfers between devices, per_device(): level_rows = lax.all_to_all(grad_blocks, 'lon', 0, 0, tiled=True)  23.8 us
    reshape x1, local copies, waits for them, and re-layouts, per_device(): block_table = full_table.reshape(2, wave_count, lon_parts, block_cols)  23 us
    all_to_all x1, waiting for transfers between devices, per_device(): level_blocks = lax.all_to_all(all_columns, 'lon', 0, 0, tiled=True)  22.3 us
    pallas_call x1, Pallas kernels, synthesis(): pl.pallas_call(synth_kernel, grid_spec=spec, out_shape=jax.ShapeDtypeStru...  15.3 us
    all_to_all x1, waiting for transfers between devices, all_reduce(): parts = lax.all_to_all(flat.reshape(count, chunk), axes, 0, 0, tiled=True)  15.2 us
    pallas_call x1, Pallas kernels, analysis(): pl.pallas_call(analyse_kernel, grid_spec=spec, out_shape=jax.ShapeDtypeSt...  14.8 us
    pallas_call x1, Pallas kernels, fourier_table(): pl.pallas_call(table_kernel, grid=(count // rows,), in_specs=[pl.BlockSpe...  12.7 us
  transfers between devices with their start and end apart: 6, of which 6 were waited for; matrix products, arithmetic and copies ran while one was open for 22% of the time, Pallas kernels for 4%

profile of v2, /device:TPU:0, one launch (start us, length us, event | category | flops | bytes accessed | tf_op | source)
XLA Modules:
  0.0 307.3 jit_solution(13727130491895307329)
XLA Ops:
  2.1 15.3 %shard_map.128 = bf16[80,128,96]{2,1,0:T(8,128)(2,1)} custom-call(s32[80]{0:T(128)} %dynamic_slice.3.ids_ref, bf16[80,96,1408]{2,1,0:T(8,128)(2,1)} %spec_ref.1, bf16[80,32,1408]{2,1,0:T(8,128)(2,1)} %basis_ref.3), custom_call_target="tpu_custom_call" | custom-call | tf_op jit(solution)/shard_map/pallas_call | solution.py:143
  26.3 7.8 %all-to-all-start = ((bf16[160,8,768]{2,0,1:T(8,128)(2,1)}), bf16[160,8,768]{2,0,1:T(8,128)(2,1)S(1)}, u32[]{:S(2)}, u32[]{:S(2)}) async-start(bf16[160,8,768]{2,0,1:T(8,128)(2,1)} %copy.84), calls=%async_computation | async-start | bytes 3932160 | tf_op jit(solution)/shard_map/all_to_all | solution.py:193
  36.3 4.0 %fusion.27 = (f32[1280,128]{1,0:T(8,128)}, f32[1280,128]{1,0:T(8,128)}) fusion(s32[1280]{0:T(1024)S(1)} %mul.94), kind=kLoop, calls=%fused_computation.40 | loop fusion | flops 1474560 | bytes 1315840 | tf_op jit(solution)/shard_map/sin | solution.py:50
  43.5 12.7 %shard_map.127 = bf16[2,1280,2560]{2,1,0:T(8,128)(2,1)} custom-call(f32[1280,20]{1,0:T(8,128)} %get-tuple-element.9.cos_a_ref, f32[1280,20]{1,0:T(8,128)} %get-tuple-element.8.sin_a_ref, f32[1280,128]{1,0:T(8,128)} %get-tuple-element.11.cos_b_ref, f32[1280,128]{1,0:T(8,128)} %get-tuple-element.10.sin_b_ref, f32[1280,1]{1,0:T(8,128)} %select_n.46.factor_ref), custom_call_target="tpu_custom_call" | custom-call | tf_op jit(solution)/shard_map/pallas_call | solution.py:56
  56.2 23.0 %reshape.109 = bf16[2,1280,4,640]{3,2,1,0:T(4,128)(2,1)} reshape(bf16[2,1280,2560]{2,1,0:T(8,128)(2,1)} %shard_map.127) | data formatting | bytes 26214400 | tf_op jit(solution)/shard_map/reshape | solution.py:199
  80.8 4.1 %copy.85 = bf16[8,160,768]{1,0,2:T(8,128)(2,1)S(1)} copy(bf16[8,160,768]{2,1,0:T(8,128)(2,1)} %bitcast.112) | data formatting | bytes 3932160 | tf_op jit(solution)/shard_map/all_to_all | solution.py:193
  84.9 5.2 %reshape.111 = bf16[1280,8,48,2]{0,3,2,1:T(2,128)(2,1)} reshape(bf16[8,160,768]{1,0,2:T(8,128)(2,1)S(1)} %copy.85) | data formatting | bytes 3932160 | tf_op jit(solution)/shard_map/reshape | solution.py:195
  90.1 11.8 %fusion.18 = bf16[4,8,48,640]{3,2,1,0:T(8,128)(2,1)} fusion(bf16[1280,8,48,2]{0,3,2,1:T(2,128)(2,1)} %reshape.111, bf16[2,1280,4,640,1]{3,2,1,0,4:T(4,128)(2,1)} %bitcast.108), kind=kOutput, calls=%fused_computation.29 | convolution fusion | flops 5034147840 | bytes 17039360 | tf_op jit(solution)/shard_map/glkc,cgbn->blkn/dot_general | solution.py:200
  101.9 3.9 %all-to-all-start.1 = ((bf16[4,8,48,640]{3,2,1,0:T(8,128)(2,1)}), bf16[4,8,48,640]{3,2,1,0:T(8,128)(2,1)S(1)}, u32[]{:S(2)}, u32[]{:S(2)}) async-start(bf16[4,8,48,640]{3,2,1,0:T(8,128)(2,1)} %fusion.18), calls=%async_computation.1 | async-start | bytes 3932160 | tf_op jit(solution)/shard_map/all_to_all | solution.py:203
  107.7 22.3 %all-to-all-done.1 = bf16[4,8,48,640]{3,2,1,0:T(8,128)(2,1)S(1)} async-done(((bf16[4,8,48,640]{3,2,1,0:T(8,128)(2,1)}), bf16[4,8,48,640]{3,2,1,0:T(8,128)(2,1)S(1)}, u32[]{:S(2)}, u32[]{:S(2)}) %all-to-all-start.1) | async-done | bytes 1966112 | tf_op jit(solution)/shard_map/all_to_all | solution.py:203
  130.3 3.8 %multiply_convert_fusion = (bf16[8,640,512]{2,1,0:T(8,128)(2,1)S(1)}, f32[8,640,512]{2,1,0:T(8,128)S(1)}) fusion(f32[512]{0:T(512)S(1)} %copy-done.6, bf16[8,192,640]{2,1,0:T(8,128)(2,1)S(1)} %bitcast.115, bf16[192,512]{1,0:T(8,128)(2,1)S(1)} %copy-done), kind=kOutput, calls=%fused_computation.15 | convolution fusion | flops 1032847360 | bytes 17893376 | tf_op jit(solution)/shard_map/lkc,kh->lch/dot_general | solution.py:206
  134.1 8.7 %convert_reduce_fusion = (f32[512]{0:T(512)S(1)}, bf16[8,640,512]{2,1,0:T(8,128)(2,1)S(1)}) fusion(f32[8,640,512]{2,1,0:T(8,128)S(1)} %get-tuple-element.13, f32[512]{0:T(512)S(1)} %copy-done.6, bf16[8,192,640]{2,1,0:T(8,128)(2,1)S(1)} %copy-done.3, bf16[512,192]{0,1:T(8,128)(2,1)S(1)} %copy-done.5), kind=kOutput, calls=%fused_computation.14 | convolution fusion | flops 1066925568 | bytes 17895424 | tf_op jit(solution)/shard_map/lkc,hk->lch/dot_general | solution.py:218
  147.5 4.7 %all-to-all-start.4 = ((f32[32,1,6272]{2,1,0:T(1,128)}), f32[32,1,6272]{2,1,0:T(1,128)S(1)}, u32[]{:S(2)}, u32[]{:S(2)}) async-start(f32[32,1,6272]{2,1,0:T(1,128)} %bitcast.32), calls=%async_computation.4 | async-start | bytes 1605632 | tf_op jit(solution)/shard_map/all_to_all | solution.py:78
  152.2 4.3 %convolution_convert_fusion.1 = bf16[8,640,192]{1,2,0:T(8,128)(2,1)S(1)} fusion(bf16[8,640,512]{2,1,0:T(8,128)(2,1)} %copy-done.2, bf16[192,512]{1,0:T(8,128)(2,1)S(1)} %copy-done), kind=kOutput, calls=%fused_computation.27 | convolution fusion | flops 1007616000 | bytes 7405568 | tf_op jit(solution)/shard_map/lch,kh->lkc/dot_general | solution.py:224
  158.0 15.2 %all-to-all-done.4 = f32[32,1,6272]{2,1,0:T(1,128)S(1)} async-done(((f32[32,1,6272]{2,1,0:T(1,128)}), f32[32,1,6272]{2,1,0:T(1,128)S(1)}, u32[]{:S(2)}, u32[]{:S(2)}) %all-to-all-start.4) | async-done | bytes 802848 | tf_op jit(solution)/shard_map/all_to_all | solution.py:78
  177.3 23.8 %all-to-all-done.2 = bf16[4,8,48,640]{3,2,1,0:T(8,128)(2,1)S(1)} async-done(((bf16[4,8,48,640]{3,2,1,0:T(8,128)(2,1)}), bf16[4,8,48,640]{3,2,1,0:T(8,128)(2,1)S(1)}, u32[]{:S(2)}, u32[]{:S(2)}) %all-to-all-start.2) | async-done | bytes 1966112 | tf_op jit(solution)/shard_map/all_to_all | solution.py:248
  205.9 8.4 %fusion.11 = bf16[1280,8,48,2]{0,2,3,1:T(8,128)(2,1)S(1)} fusion(bf16[2,160,4,8,640]{4,3,2,1,0:T(8,128)(2,1)} %bitcast.107, bf16[4,8,48,640]{3,2,1,0:T(8,128)(2,1)S(1)} %all-to-all-done.2), kind=kOutput, calls=%fused_computation.20 | convolution fusion | flops 5034147840 | bytes 17039360 | tf_op jit(solution)/shard_map/cgbn,blkn->glkc/dot_general | solution.py:249
  217.1 6.4 %all_to_all.45 = bf16[8,160,768]{1,0,2:T(8,128)(2,1)S(1)} reshape(bf16[1280,8,48,2]{0,3,2,1:T(2,128)(2,1)} %copy.92) | data formatting | bytes 3932160 | tf_op jit(solution)/shard_map/all_to_all | solution.py:253
  226.9 6.2 %all-to-all-start.3 = ((bf16[8,160,768]{2,1,0:T(8,128)(2,1)}), bf16[8,160,768]{2,1,0:T(8,128)(2,1)S(1)}, u32[]{:S(2)}, u32[]{:S(2)}) async-start(bf16[8,160,768]{2,1,0:T(8,128)(2,1)} %copy.93), calls=%async_computation.3 | async-start | bytes 3932160 | tf_op jit(solution)/shard_map/all_to_all | solution.py:253
  233.0 5.6 %fusion.17 = bf16[8,192,640]{2,1,0:T(8,128)(2,1)} fusion(f32[192]{0:T(256)S(1)} %copy-done.7, bf16[8,640,512]{2,1,0:T(8,128)(2,1)} %copy-done.8, bf16[512,192]{0,1:T(8,128)(2,1)S(1)} %copy-done.5), kind=kOutput, calls=%fused_computation.28 | convolution fusion | flops 1008599040 | bytes 7406336 | tf_op jit(solution)/shard_map/lch,hk->lkc/dot_general | solution.py:211
  247.4 31.3 %all-to-all-done.3 = bf16[8,160,768]{2,1,0:T(8,128)(2,1)S(1)} async-done(((bf16[8,160,768]{2,1,0:T(8,128)(2,1)}), bf16[8,160,768]{2,1,0:T(8,128)(2,1)S(1)}, u32[]{:S(2)}, u32[]{:S(2)}) %all-to-all-start.3) | async-done | bytes 1966112 | tf_op jit(solution)/shard_map/all_to_all | solution.py:253
  281.1 4.6 %reshape.114 = bf16[80,2,64,96]{3,2,1,0:T(8,128)(2,1)S(1)} reshape(bf16[160,8,768]{2,1,0:T(8,128)(2,1)} %copy.94) | data formatting | bytes 3932160 | tf_op jit(solution)/shard_map/reshape | solution.py:254
  287.9 4.3 %copy.95.grad_ref = bf16[80,96,128]{2,1,0:T(8,128)(2,1)} copy(bf16[80,96,128]{1,2,0:T(8,128)(2,1)} %bitcast.110) | data formatting | bytes 3932160 | tf_op jit(solution)/shard_map/reshape | solution.py:257
  292.2 14.8 %shard_map.129 = bf16[80,96,1408]{2,1,0:T(8,128)(2,1)} custom-call(s32[80]{0:T(128)} %dynamic_slice.3.ids_ref, bf16[80,96,128]{2,1,0:T(8,128)(2,1)} %copy.95.grad_ref, bf16[80,32,1408]{2,1,0:T(8,128)(2,1)} %basis_ref.3), custom_call_target="tpu_custom_call" | custom-call | tf_op jit(solution)/shard_map/pallas_call | solution.py:164
  (59 shorter events, 53.8 us)
Async XLA Ops:
  0.6 129.6 %copy-start = (bf16[192,512]{1,0:T(8,128)(2,1)S(1)}, bf16[192,512]{1,0:T(8,128)(2,1)}, u32[]{:S(2)}) copy-start(bf16[192,512]{1,0:T(8,128)(2,1)} %param.11) | copy-start | bytes 589828
  20.0 14.2 %copy-start.4 = (s32[640]{0:T(1024)S(1)}, s32[640]{0:T(1024)}, u32[]{:S(2)}) copy-start(s32[640]{0:T(1024)} %param.8) | copy-start | bytes 7684
  26.3 53.2 %all-to-all-start = ((bf16[160,8,768]{2,0,1:T(8,128)(2,1)}), bf16[160,8,768]{2,0,1:T(8,128)(2,1)S(1)}, u32[]{:S(2)}, u32[]{:S(2)}) async-start(bf16[160,8,768]{2,0,1:T(8,128)(2,1)} %copy.84), calls=%async_computation | async-start | bytes 3932160 | tf_op jit(solution)/shard_map/all_to_all | solution.py:193
  79.5 1.3 copy-start.1
  101.9 28.4 %copy-start.6 = (f32[512]{0:T(512)S(1)}, f32[512]{0:T(512)}, u32[]{:S(2)}) copy-start(f32[512]{0:T(512)} %param.12) | copy-start | bytes 6148
  101.9 28.2 %all-to-all-start.1 = ((bf16[4,8,48,640]{3,2,1,0:T(8,128)(2,1)}), bf16[4,8,48,640]{3,2,1,0:T(8,128)(2,1)S(1)}, u32[]{:S(2)}, u32[]{:S(2)}) async-start(bf16[4,8,48,640]{3,2,1,0:T(8,128)(2,1)} %fusion.18), calls=%async_computation.1 | async-start | bytes 3932160 | tf_op jit(solution)/shard_map/all_to_all | solution.py:203
  130.3 3.8 %copy-start.3 = (bf16[8,192,640]{2,1,0:T(8,128)(2,1)S(1)}, bf16[8,192,640]{2,1,0:T(8,128)(2,1)}, u32[]{:S(2)}) copy-start(bf16[8,192,640]{2,1,0:T(8,128)(2,1)} %param.15) | copy-start | bytes 5898244
  130.3 3.8 %copy-start.5 = (bf16[512,192]{0,1:T(8,128)(2,1)S(1)}, bf16[512,192]{0,1:T(8,128)(2,1)}, u32[]{:S(2)}) copy-start(bf16[512,192]{0,1:T(8,128)(2,1)} %param.13) | copy-start | bytes 589828
  134.1 11.1 %copy-start.8 = (bf16[8,640,512]{2,1,0:T(8,128)(2,1)}, bf16[8,640,512]{2,1,0:T(8,128)(2,1)S(1)}, u32[]{:S(2)}) copy-start(bf16[8,640,512]{2,1,0:T(8,128)(2,1)S(1)} %get-tuple-element.12) | copy-start | bytes 15728644
  142.8 2.3 copy-start.2
  147.5 25.7 %all-to-all-start.4 = ((f32[32,1,6272]{2,1,0:T(1,128)}), f32[32,1,6272]{2,1,0:T(1,128)S(1)}, u32[]{:S(2)}, u32[]{:S(2)}) async-start(f32[32,1,6272]{2,1,0:T(1,128)} %bitcast.32), calls=%async_computation.4 | async-start | bytes 1605632 | tf_op jit(solution)/shard_map/all_to_all | solution.py:78
  173.2 27.9 %all-to-all-start.2 = ((bf16[4,8,48,640]{3,2,1,0:T(8,128)(2,1)}), bf16[4,8,48,640]{3,2,1,0:T(8,128)(2,1)S(1)}, u32[]{:S(2)}, u32[]{:S(2)}) async-start(bf16[4,8,48,640]{3,2,1,0:T(8,128)(2,1)} %bitcast.106), calls=%async_computation.2 | async-start | bytes 3932160 | tf_op jit(solution)/shard_map/all_to_all | solution.py:248
  202.4 24.5 %all-to-all-start.5 = ((f32[32,1,6272]{2,1,0:T(1,128)}), f32[32,1,6272]{2,1,0:T(1,128)}, u32[]{:S(2)}, u32[]{:S(2)}) async-start(f32[32,1,6272]{2,1,0:T(1,128)} %broadcast_in_dim.31), calls=%async_computation.5 | async-start | bytes 1605632 | tf_op jit(solution)/shard_map/all_to_all | solution.py:81
  223.5 9.5 %copy-start.7 = (f32[192]{0:T(256)S(1)}, f32[192]{0:T(256)}, u32[]{:S(2)}) copy-start(f32[192]{0:T(256)} %param.14) | copy-start | bytes 2308
  226.9 51.9 %all-to-all-start.3 = ((bf16[8,160,768]{2,1,0:T(8,128)(2,1)}), bf16[8,160,768]{2,1,0:T(8,128)(2,1)S(1)}, u32[]{:S(2)}, u32[]{:S(2)}) async-start(bf16[8,160,768]{2,1,0:T(8,128)(2,1)} %copy.93), calls=%async_computation.3 | async-start | bytes 3932160 | tf_op jit(solution)/shard_map/all_to_all | solution.py:253

commit v3 on v2

--- a/solution.py
+++ b/solution.py
@@ -75,8 +75,9 @@
     flat = value.reshape(-1)
     chunk = -(-flat.shape[0] // (count * 128)) * 128
     flat = jnp.pad(flat, (0, chunk * count - flat.shape[0]))
-    parts = lax.all_to_all(flat.reshape(count, chunk), axes, 0, 0, tiled=True)
-    owned = jnp.sum(parts, axis=0, keepdims=True)
+    sent = flat.reshape(count, chunk).astype(jnp.bfloat16)
+    parts = lax.all_to_all(sent, axes, 0, 0, tiled=True)
+    owned = jnp.sum(parts.astype(jnp.float32), axis=0, keepdims=True)
     spread = jnp.broadcast_to(owned, (count, chunk))
     whole = lax.all_to_all(spread, axes, 0, 0, tiled=True).reshape(-1)
     return whole[: value.size].reshape(value.shape)

time: 313 us -> 309 us (0.987)
  waiting for transfers between devices: 93.1 us -> 84.8 us
  other arithmetic: 12.8 us -> 16.1 us
    all_to_all x1, waiting for transfers between devices: 15.2 us -> 7.68 us  [all_reduce(): parts = lax.all_to_all(sent, axes, 0, 0, tiled=True)]
  transfers between devices with their start and end apart: 6 -> 6, of which waited for: 6 -> 6; matrix products, arithmetic and copies ran while one was open for 22% -> 23% of each run, Pallas kernels for 4% -> 4%
where the time goes in v3:
time: 309 us; the launch traced here: 304 us
  waiting for transfers between devices  84.8 us (27%)
  local copies, waits for them, and re-layouts  79.1 us (26%)
  matrix products  49.9 us (16%)
  Pallas kernels  42.9 us (14%)
  starting transfers between devices  29.5 us (10%)
  other arithmetic  16.1 us (5%)
    all_to_all x1, waiting for transfers between devices, per_device(): lax.all_to_all(flat_grad, 'lat', split_axis=0, concat_axis=1, tiled=True)  31.3 us
    all_to_all x1, waiting for transfers between devices, per_device(): level_rows = lax.all_to_all(grad_blocks, 'lon', 0, 0, tiled=True)  23 us
    reshape x1, local copies, waits for them, and re-layouts, per_device(): block_table = full_table.reshape(2, wave_count, lon_parts, block_cols)  23 us
    all_to_all x1, waiting for transfers between devices, per_device(): level_blocks = lax.all_to_all(all_columns, 'lon', 0, 0, tiled=True)  22.3 us
    pallas_call x1, Pallas kernels, synthesis(): pl.pallas_call(synth_kernel, grid_spec=spec, out_shape=jax.ShapeDtypeStru...  15.3 us
    pallas_call x1, Pallas kernels, analysis(): pl.pallas_call(analyse_kernel, grid_spec=spec, out_shape=jax.ShapeDtypeSt...  14.8 us
    pallas_call x1, Pallas kernels, fourier_table(): pl.pallas_call(table_kernel, grid=(count // rows,), in_specs=[pl.BlockSpe...  12.7 us
    all_to_all x3, local copies, waits for them, and re-layouts, per_device(): lax.all_to_all(flat_grad, 'lat', split_axis=0, concat_axis=1, tiled=True)  12 us
  transfers between devices with their start and end apart: 6, of which 6 were waited for; matrix products, arithmetic and copies ran while one was open for 23% of the time, Pallas kernels for 4%

profile of v3, /device:TPU:0, one launch (start us, length us, event | category | flops | bytes accessed | tf_op | source)
XLA Modules:
  0.0 303.6 jit_solution(11309732429323430850)
XLA Ops:
  2.0 15.3 %shard_map.128 = bf16[80,128,96]{2,1,0:T(8,128)(2,1)} custom-call(s32[80]{0:T(128)} %dynamic_slice.3.ids_ref, bf16[80,96,1408]{2,1,0:T(8,128)(2,1)} %spec_ref.1, bf16[80,32,1408]{2,1,0:T(8,128)(2,1)} %basis_ref.3), custom_call_target="tpu_custom_call" | custom-call | tf_op jit(solution)/shard_map/pallas_call | solution.py:144
  26.3 7.8 %all-to-all-start = ((bf16[160,8,768]{2,0,1:T(8,128)(2,1)}), bf16[160,8,768]{2,0,1:T(8,128)(2,1)S(1)}, u32[]{:S(2)}, u32[]{:S(2)}) async-start(bf16[160,8,768]{2,0,1:T(8,128)(2,1)} %copy.52), calls=%async_computation | async-start | bytes 3932160 | tf_op jit(solution)/shard_map/all_to_all | solution.py:194
  36.2 4.0 %fusion.31 = (f32[1280,128]{1,0:T(8,128)}, f32[1280,128]{1,0:T(8,128)}) fusion(s32[1280]{0:T(1024)S(1)} %mul.94), kind=kLoop, calls=%fused_computation.42 | loop fusion | flops 1474560 | bytes 1315840 | tf_op jit(solution)/shard_map/sin | solution.py:50
  43.4 12.7 %shard_map.127 = bf16[2,1280,2560]{2,1,0:T(8,128)(2,1)} custom-call(f32[1280,20]{1,0:T(8,128)} %get-tuple-element.9.cos_a_ref, f32[1280,20]{1,0:T(8,128)} %get-tuple-element.8.sin_a_ref, f32[1280,128]{1,0:T(8,128)} %get-tuple-element.11.cos_b_ref, f32[1280,128]{1,0:T(8,128)} %get-tuple-element.10.sin_b_ref, f32[1280,1]{1,0:T(8,128)} %select_n.46.factor_ref), custom_call_target="tpu_custom_call" | custom-call | tf_op jit(solution)/shard_map/pallas_call | solution.py:56
  56.1 23.0 %reshape.121 = bf16[2,1280,4,640]{3,2,1,0:T(4,128)(2,1)} reshape(bf16[2,1280,2560]{2,1,0:T(8,128)(2,1)} %shard_map.127) | data formatting | bytes 26214400 | tf_op jit(solution)/shard_map/reshape | solution.py:200
  80.7 4.1 %copy.53 = bf16[8,160,768]{1,0,2:T(8,128)(2,1)S(1)} copy(bf16[8,160,768]{2,1,0:T(8,128)(2,1)} %bitcast.115) | data formatting | bytes 3932160 | tf_op jit(solution)/shard_map/all_to_all | solution.py:194
  84.8 5.2 %reshape.123 = bf16[1280,8,48,2]{0,3,2,1:T(2,128)(2,1)} reshape(bf16[8,160,768]{1,0,2:T(8,128)(2,1)S(1)} %copy.53) | data formatting | bytes 3932160 | tf_op jit(solution)/shard_map/reshape | solution.py:196
  90.1 11.8 %fusion.18 = bf16[4,8,48,640]{3,2,1,0:T(8,128)(2,1)} fusion(bf16[1280,8,48,2]{0,3,2,1:T(2,128)(2,1)} %reshape.123, bf16[2,1280,4,640,1]{3,2,1,0,4:T(4,128)(2,1)} %bitcast.111), kind=kOutput, calls=%fused_computation.27 | convolution fusion | flops 5034147840 | bytes 17039360 | tf_op jit(solution)/shard_map/glkc,cgbn->blkn/dot_general | solution.py:201
  101.9 3.9 %all-to-all-start.1 = ((bf16[4,8,48,640]{3,2,1,0:T(8,128)(2,1)}), bf16[4,8,48,640]{3,2,1,0:T(8,128)(2,1)S(1)}, u32[]{:S(2)}, u32[]{:S(2)}) async-start(bf16[4,8,48,640]{3,2,1,0:T(8,128)(2,1)} %fusion.18), calls=%async_computation.1 | async-start | bytes 3932160 | tf_op jit(solution)/shard_map/all_to_all | solution.py:204
  107.7 22.3 %all-to-all-done.1 = bf16[4,8,48,640]{3,2,1,0:T(8,128)(2,1)S(1)} async-done(((bf16[4,8,48,640]{3,2,1,0:T(8,128)(2,1)}), bf16[4,8,48,640]{3,2,1,0:T(8,128)(2,1)S(1)}, u32[]{:S(2)}, u32[]{:S(2)}) %all-to-all-start.1) | async-done | bytes 1966112 | tf_op jit(solution)/shard_map/all_to_all | solution.py:204
  130.3 3.8 %multiply_convert_fusion = (bf16[8,640,512]{2,1,0:T(8,128)(2,1)S(1)}, f32[8,640,512]{2,1,0:T(8,128)S(1)}) fusion(f32[512]{0:T(512)S(1)} %copy-done.6, bf16[8,192,640]{2,1,0:T(8,128)(2,1)S(1)} %bitcast.118, bf16[192,512]{1,0:T(8,128)(2,1)S(1)} %copy-done), kind=kOutput, calls=%fused_computation.14 | convolution fusion | flops 1032847360 | bytes 17893376 | tf_op jit(solution)/shard_map/lkc,kh->lch/dot_general | solution.py:207
  134.1 8.7 %fusion.49 = (bf16[512]{0:T(512)(128)(2,1)S(1)}, bf16[8,640,512]{2,1,0:T(8,128)(2,1)S(1)}) fusion(f32[8,640,512]{2,1,0:T(8,128)S(1)} %get-tuple-element.13, f32[512]{0:T(512)S(1)} %copy-done.6, bf16[8,192,640]{2,1,0:T(8,128)(2,1)S(1)} %copy-done.3, bf16[512,192]{0,1:T(8,128)(2,1)S(1)} %copy-done.5), kind=kOutput, calls=%fused_computation.69 | convolution fusion | flops 1064304128 | bytes 17894400 | tf_op jit(solution)/shard_map/lkc,hk->lch/dot_general | solution.py:219
  151.5 4.9 %all-to-all-start.4 = ((bf16[32,2,3136]{2,1,0:T(2,128)(2,1)}), bf16[32,2,3136]{2,1,0:T(2,128)(2,1)S(1)}, u32[]{:S(2)}, u32[]{:S(2)}) async-start(bf16[32,2,3136]{2,1,0:T(2,128)(2,1)} %reshape.143), calls=%async_computation.4 | async-start | bytes 819200 | tf_op jit(solution)/shard_map/all_to_all | solution.py:79
  156.4 4.3 %convolution_convert_fusion.1 = bf16[8,640,192]{1,2,0:T(8,128)(2,1)S(1)} fusion(bf16[8,640,512]{2,1,0:T(8,128)(2,1)} %copy-done.2, bf16[192,512]{1,0:T(8,128)(2,1)S(1)} %copy-done), kind=kOutput, calls=%fused_computation.25 | convolution fusion | flops 1007616000 | bytes 7405568 | tf_op jit(solution)/shard_map/lch,kh->lkc/dot_general | solution.py:225
  162.2 7.7 %all-to-all-done.4 = bf16[32,2,3136]{2,1,0:T(2,128)(2,1)S(1)} async-done(((bf16[32,2,3136]{2,1,0:T(2,128)(2,1)}), bf16[32,2,3136]{2,1,0:T(2,128)(2,1)S(1)}, u32[]{:S(2)}, u32[]{:S(2)}) %all-to-all-start.4) | async-done | bytes 401440 | tf_op jit(solution)/shard_map/all_to_all | solution.py:79
  174.8 23.0 %all-to-all-done.2 = bf16[4,8,48,640]{3,2,1,0:T(8,128)(2,1)S(1)} async-done(((bf16[4,8,48,640]{3,2,1,0:T(8,128)(2,1)}), bf16[4,8,48,640]{3,2,1,0:T(8,128)(2,1)S(1)}, u32[]{:S(2)}, u32[]{:S(2)}) %all-to-all-start.2) | async-done | bytes 1966112 | tf_op jit(solution)/shard_map/all_to_all | solution.py:249
  202.4 8.4 %fusion.11 = bf16[1280,8,48,2]{0,2,3,1:T(8,128)(2,1)S(1)} fusion(bf16[2,160,4,8,640]{4,3,2,1,0:T(8,128)(2,1)} %bitcast.110, bf16[4,8,48,640]{3,2,1,0:T(8,128)(2,1)S(1)} %all-to-all-done.2), kind=kOutput, calls=%fused_computation.18 | convolution fusion | flops 5034147840 | bytes 17039360 | tf_op jit(solution)/shard_map/cgbn,blkn->glkc/dot_general | solution.py:250
  213.6 6.4 %all_to_all.43 = bf16[8,160,768]{1,0,2:T(8,128)(2,1)S(1)} reshape(bf16[1280,8,48,2]{0,3,2,1:T(2,128)(2,1)} %copy.60) | data formatting | bytes 3932160 | tf_op jit(solution)/shard_map/all_to_all | solution.py:254
  223.4 6.0 %all-to-all-start.3 = ((bf16[8,160,768]{2,1,0:T(8,128)(2,1)}), bf16[8,160,768]{2,1,0:T(8,128)(2,1)S(1)}, u32[]{:S(2)}, u32[]{:S(2)}) async-start(bf16[8,160,768]{2,1,0:T(8,128)(2,1)} %copy.61), calls=%async_computation.3 | async-start | bytes 3932160 | tf_op jit(solution)/shard_map/all_to_all | solution.py:254
  229.3 5.6 %fusion.17 = bf16[8,192,640]{2,1,0:T(8,128)(2,1)} fusion(f32[192]{0:T(256)S(1)} %copy-done.7, bf16[8,640,512]{2,1,0:T(8,128)(2,1)} %copy-done.8, bf16[512,192]{0,1:T(8,128)(2,1)} %param.13), kind=kOutput, calls=%fused_computation.26 | convolution fusion | flops 1008599040 | bytes 7406336 | tf_op jit(solution)/shard_map/lch,hk->lkc/dot_general | solution.py:212
  243.7 31.3 %all-to-all-done.3 = bf16[8,160,768]{2,1,0:T(8,128)(2,1)S(1)} async-done(((bf16[8,160,768]{2,1,0:T(8,128)(2,1)}), bf16[8,160,768]{2,1,0:T(8,128)(2,1)S(1)}, u32[]{:S(2)}, u32[]{:S(2)}) %all-to-all-start.3) | async-done | bytes 1966112 | tf_op jit(solution)/shard_map/all_to_all | solution.py:254
  277.4 4.6 %reshape.126 = bf16[80,2,64,96]{3,2,1,0:T(8,128)(2,1)S(1)} reshape(bf16[160,8,768]{2,1,0:T(8,128)(2,1)} %copy.62) | data formatting | bytes 3932160 | tf_op jit(solution)/shard_map/reshape | solution.py:255
  284.3 4.2 %copy.63.grad_ref = bf16[80,96,128]{2,1,0:T(8,128)(2,1)} copy(bf16[80,96,128]{1,2,0:T(8,128)(2,1)} %bitcast.113) | data formatting | bytes 3932160 | tf_op jit(solution)/shard_map/reshape | solution.py:258
  288.5 14.8 %shard_map.129 = bf16[80,96,1408]{2,1,0:T(8,128)(2,1)} custom-call(s32[80]{0:T(128)} %dynamic_slice.3.ids_ref, bf16[80,96,128]{2,1,0:T(8,128)(2,1)} %copy.63.grad_ref, bf16[80,32,1408]{2,1,0:T(8,128)(2,1)} %basis_ref.3), custom_call_target="tpu_custom_call" | custom-call | tf_op jit(solution)/shard_map/pallas_call | solution.py:165
  (66 shorter events, 58.5 us)
Async XLA Ops:
  0.6 129.6 %copy-start = (bf16[192,512]{1,0:T(8,128)(2,1)S(1)}, bf16[192,512]{1,0:T(8,128)(2,1)}, u32[]{:S(2)}) copy-start(bf16[192,512]{1,0:T(8,128)(2,1)} %param.11) | copy-start | bytes 589828
  20.0 14.1 %copy-start.4 = (s32[640]{0:T(1024)S(1)}, s32[640]{0:T(1024)}, u32[]{:S(2)}) copy-start(s32[640]{0:T(1024)} %param.8) | copy-start | bytes 7684
  26.3 53.1 %all-to-all-start = ((bf16[160,8,768]{2,0,1:T(8,128)(2,1)}), bf16[160,8,768]{2,0,1:T(8,128)(2,1)S(1)}, u32[]{:S(2)}, u32[]{:S(2)}) async-start(bf16[160,8,768]{2,0,1:T(8,128)(2,1)} %copy.52), calls=%async_computation | async-start | bytes 3932160 | tf_op jit(solution)/shard_map/all_to_all | solution.py:194
  79.5 1.3 copy-start.1
  101.9 28.4 %copy-start.6 = (f32[512]{0:T(512)S(1)}, f32[512]{0:T(512)}, u32[]{:S(2)}) copy-start(f32[512]{0:T(512)} %param.12) | copy-start | bytes 6148
  101.9 28.2 %all-to-all-start.1 = ((bf16[4,8,48,640]{3,2,1,0:T(8,128)(2,1)}), bf16[4,8,48,640]{3,2,1,0:T(8,128)(2,1)S(1)}, u32[]{:S(2)}, u32[]{:S(2)}) async-start(bf16[4,8,48,640]{3,2,1,0:T(8,128)(2,1)} %fusion.18), calls=%async_computation.1 | async-start | bytes 3932160 | tf_op jit(solution)/shard_map/all_to_all | solution.py:204
  130.3 3.8 %copy-start.3 = (bf16[8,192,640]{2,1,0:T(8,128)(2,1)S(1)}, bf16[8,192,640]{2,1,0:T(8,128)(2,1)}, u32[]{:S(2)}) copy-start(bf16[8,192,640]{2,1,0:T(8,128)(2,1)} %param.15) | copy-start | bytes 5898244
  130.3 3.8 %copy-start.5 = (bf16[512,192]{0,1:T(8,128)(2,1)S(1)}, bf16[512,192]{0,1:T(8,128)(2,1)}, u32[]{:S(2)}) copy-start(bf16[512,192]{0,1:T(8,128)(2,1)} %param.13) | copy-start | bytes 589828
  134.1 11.1 %copy-start.8 = (bf16[8,640,512]{2,1,0:T(8,128)(2,1)}, bf16[8,640,512]{2,1,0:T(8,128)(2,1)S(1)}, u32[]{:S(2)}) copy-start(bf16[8,640,512]{2,1,0:T(8,128)(2,1)S(1)} %get-tuple-element.12) | copy-start | bytes 15728644
  142.8 2.3 copy-start.2
  151.5 18.4 %all-to-all-start.4 = ((bf16[32,2,3136]{2,1,0:T(2,128)(2,1)}), bf16[32,2,3136]{2,1,0:T(2,128)(2,1)S(1)}, u32[]{:S(2)}, u32[]{:S(2)}) async-start(bf16[32,2,3136]{2,1,0:T(2,128)(2,1)} %reshape.143), calls=%async_computation.4 | async-start | bytes 819200 | tf_op jit(solution)/shard_map/all_to_all | solution.py:79
  169.9 27.9 %all-to-all-start.2 = ((bf16[4,8,48,640]{3,2,1,0:T(8,128)(2,1)}), bf16[4,8,48,640]{3,2,1,0:T(8,128)(2,1)S(1)}, u32[]{:S(2)}, u32[]{:S(2)}) async-start(bf16[4,8,48,640]{3,2,1,0:T(8,128)(2,1)} %bitcast.109), calls=%async_computation.2 | async-start | bytes 3932160 | tf_op jit(solution)/shard_map/all_to_all | solution.py:249
  199.1 24.3 %all-to-all-start.5 = ((f32[32,1,6272]{2,1,0:T(1,128)}), f32[32,1,6272]{2,1,0:T(1,128)}, u32[]{:S(2)}, u32[]{:S(2)}) async-start(f32[32,1,6272]{2,1,0:T(1,128)} %broadcast_in_dim.33), calls=%async_computation.5 | async-start | bytes 1605632 | tf_op jit(solution)/shard_map/all_to_all | solution.py:82
  220.0 9.3 %copy-start.7 = (f32[192]{0:T(256)S(1)}, f32[192]{0:T(256)}, u32[]{:S(2)}) copy-start(f32[192]{0:T(256)} %param.14) | copy-start | bytes 2308
  223.4 51.7 %all-to-all-start.3 = ((bf16[8,160,768]{2,1,0:T(8,128)(2,1)}), bf16[8,160,768]{2,1,0:T(8,128)(2,1)S(1)}, u32[]{:S(2)}, u32[]{:S(2)}) async-start(bf16[8,160,768]{2,1,0:T(8,128)(2,1)} %copy.61), calls=%async_computation.3 | async-start | bytes 3932160 | tf_op jit(solution)/shard_map/all_to_all | solution.py:254

commit v4 on v3

--- a/solution.py
+++ b/solution.py
@@ -240,13 +240,14 @@
         ],
         axis=0,
     )
+    grad_blocks = jnp.swapaxes(grid_grad.reshape(band_rows, lon_parts, -1, block_cols), 0, 1)
+    level_rows = lax.all_to_all(grad_blocks, "lon", 0, 0, tiled=True)
+    stacked, level_rows = lax.optimization_barrier((stacked, level_rows))
     summed = all_reduce(stacked, ("lat", "lon"))
     in_weight_grad = summed[:channels, :hid]
     out_weight_grad = summed[channels : 2 * channels, :hid].T
     in_bias_grad = summed[2 * channels, :hid]
     out_bias_grad = summed[2 * channels + 1, :channels]
-    grad_blocks = jnp.swapaxes(grid_grad.reshape(band_rows, lon_parts, -1, block_cols), 0, 1)
-    level_rows = lax.all_to_all(grad_blocks, "lon", 0, 0, tiled=True)
     wave_grad = jnp.einsum(
         "cgbn,blkn->glkc", block_table, level_rows, preferred_element_type=jnp.float32
     ).astype(jnp.bfloat16)

time: 309 us -> 310 us (level)
  blocking collectives: 0 us -> 45.2 us
  waiting for transfers between devices: 84.8 us -> 50 us
  starting transfers between devices: 29.5 us -> 21.6 us
    all_to_all x0 -> x2, blocking collectives: none -> 45.2 us  [the longest x1 27 us: per_device(): level_blocks = lax.all_to_all(all_columns, 'lon', 0, 0, tiled=True)]
    all_to_all x2 -> x0, waiting for transfers between devices: 30 us -> none  [the longest x1 22.3 us: per_device(): level_blocks = lax.all_to_all(all_columns, 'lon', 0, 0, tiled=True)]
    all_to_all x2 -> x0, starting transfers between devices: 8.81 us -> none  [the longest x1 4.91 us: all_reduce(): parts = lax.all_to_all(sent, axes, 0, 0, tiled=True)]
    all_to_all x1, waiting for transfers between devices: 23 us -> 18.3 us  [per_device(): level_rows = lax.all_to_all(grad_blocks, 'lon', 0, 0, tiled=True)]
    dot_general x1, matrix products: 1.18 us -> 4.44 us  [per_device(): jnp.einsum('lkc,lch->kh', grid, pre_grad, preferred_element_type=jnp.floa...]
  transfers between devices with their start and end apart: 6 -> 4, of which waited for: 6 -> 3; matrix products, arithmetic and copies ran while one was open for 23% -> 22% of each run, Pallas kernels for 4% -> 4%
where the time goes in v4:
time: 310 us; the launch traced here: 305 us
  local copies, waits for them, and re-layouts  77.2 us (25%)
  matrix products  51.8 us (17%)
  waiting for transfers between devices  50 us (16%)
  blocking collectives  45.2 us (15%)
  Pallas kernels  42.9 us (14%)
  starting transfers between devices  21.6 us (7%)
  other arithmetic  14.5 us (5%)
    all_to_all x1, waiting for transfers between devices, per_device(): lax.all_to_all(flat_grad, 'lat', split_axis=0, concat_axis=1, tiled=True)  31.3 us
    all_to_all x1, blocking collectives, per_device(): level_blocks = lax.all_to_all(all_columns, 'lon', 0, 0, tiled=True)  27 us
    reshape x1, local copies, waits for them, and re-layouts, per_device(): block_table = full_table.reshape(2, wave_count, lon_parts, block_cols)  23 us
    all_to_all x1, waiting for transfers between devices, per_device(): level_rows = lax.all_to_all(grad_blocks, 'lon', 0, 0, tiled=True)  18.3 us
    all_to_all x1, blocking collectives, all_reduce(): parts = lax.all_to_all(sent, axes, 0, 0, tiled=True)  18.2 us
    pallas_call x1, Pallas kernels, synthesis(): pl.pallas_call(synth_kernel, grid_spec=spec, out_shape=jax.ShapeDtypeStru...  15.3 us
    pallas_call x1, Pallas kernels, analysis(): pl.pallas_call(analyse_kernel, grid_spec=spec, out_shape=jax.ShapeDtypeSt...  14.8 us
    pallas_call x1, Pallas kernels, fourier_table(): pl.pallas_call(table_kernel, grid=(count // rows,), in_specs=[pl.BlockSpe...  12.7 us
  transfers between devices with their start and end apart: 4, of which 3 were waited for; matrix products, arithmetic and copies ran while one was open for 22% of the time, Pallas kernels for 4%

profile of v4, /device:TPU:0, one launch (start us, length us, event | category | flops | bytes accessed | tf_op | source)
XLA Modules:
  0.0 304.5 jit_solution(4168312914269856992)
XLA Ops:
  2.0 15.3 %shard_map.128 = bf16[80,128,96]{2,1,0:T(8,128)(2,1)} custom-call(s32[80]{0:T(128)} %dynamic_slice.3.ids_ref, bf16[80,96,1408]{2,1,0:T(8,128)(2,1)} %spec_ref.1, bf16[80,32,1408]{2,1,0:T(8,128)(2,1)} %basis_ref.3), custom_call_target="tpu_custom_call" | custom-call | tf_op jit(solution)/shard_map/pallas_call | solution.py:144
  26.3 7.8 %all-to-all-start = ((bf16[160,8,768]{2,0,1:T(8,128)(2,1)}), bf16[160,8,768]{2,0,1:T(8,128)(2,1)S(1)}, u32[]{:S(2)}, u32[]{:S(2)}) async-start(bf16[160,8,768]{2,0,1:T(8,128)(2,1)} %copy.52), calls=%async_computation | async-start | bytes 3932160 | tf_op jit(solution)/shard_map/all_to_all | solution.py:194
  36.2 4.0 %fusion.27 = (f32[1280,128]{1,0:T(8,128)}, f32[1280,128]{1,0:T(8,128)}) fusion(s32[1280]{0:T(1024)S(1)} %mul.94), kind=kLoop, calls=%fused_computation.41 | loop fusion | flops 1474560 | bytes 1315840 | tf_op jit(solution)/shard_map/sin | solution.py:50
  43.4 12.7 %shard_map.127 = bf16[2,1280,2560]{2,1,0:T(8,128)(2,1)} custom-call(f32[1280,20]{1,0:T(8,128)} %get-tuple-element.13.cos_a_ref, f32[1280,20]{1,0:T(8,128)} %get-tuple-element.12.sin_a_ref, f32[1280,128]{1,0:T(8,128)} %get-tuple-element.15.cos_b_ref, f32[1280,128]{1,0:T(8,128)} %get-tuple-element.14.sin_b_ref, f32[1280,1]{1,0:T(8,128)} %select_n.46.factor_ref), custom_call_target="tpu_custom_call" | custom-call | tf_op jit(solution)/shard_map/pallas_call | solution.py:56
  56.1 23.0 %reshape.121 = bf16[2,1280,4,640]{3,2,1,0:T(4,128)(2,1)} reshape(bf16[2,1280,2560]{2,1,0:T(8,128)(2,1)} %shard_map.127) | data formatting | bytes 26214400 | tf_op jit(solution)/shard_map/reshape | solution.py:200
  80.7 4.1 %copy.53 = bf16[8,160,768]{1,0,2:T(8,128)(2,1)S(1)} copy(bf16[8,160,768]{2,1,0:T(8,128)(2,1)} %bitcast.111) | data formatting | bytes 3932160 | tf_op jit(solution)/shard_map/all_to_all | solution.py:194
  84.8 5.2 %reshape.123 = bf16[1280,8,48,2]{0,3,2,1:T(2,128)(2,1)} reshape(bf16[8,160,768]{1,0,2:T(8,128)(2,1)S(1)} %copy.53) | data formatting | bytes 3932160 | tf_op jit(solution)/shard_map/reshape | solution.py:196
  90.1 10.5 %fusion.18 = bf16[4,8,48,640]{3,2,1,0:T(8,128)(2,1)S(1)} fusion(bf16[1280,8,48,2]{0,3,2,1:T(2,128)(2,1)} %reshape.123, bf16[2,1280,4,640,1]{3,2,1,0,4:T(4,128)(2,1)} %bitcast.107), kind=kOutput, calls=%fused_computation.29 | convolution fusion | flops 5034147840 | bytes 17039360 | tf_op jit(solution)/shard_map/glkc,cgbn->blkn/dot_general | solution.py:201
  100.6 27.0 %all_to_all.54 = bf16[4,8,48,640]{3,2,1,0:T(8,128)(2,1)S(1)} all-to-all(bf16[4,8,48,640]{3,2,1,0:T(8,128)(2,1)S(1)} %fusion.18), channel_id=1, replica_groups=mesh['lat'=8,'lon'=4] {'lon'}, dimensions={0} | all-to-all | bytes 3932160 | tf_op jit(solution)/shard_map/all_to_all | solution.py:204
  127.9 5.5 %multiply_convert_fusion = (bf16[8,640,512]{2,1,0:T(8,128)(2,1)}, f32[8,640,512]{2,1,0:T(8,128)S(1)}) fusion(f32[512]{0:T(512)S(1)} %copy-done.7, bf16[8,192,640]{2,1,0:T(8,128)(2,1)S(1)} %bitcast.114, bf16[192,512]{1,0:T(8,128)(2,1)S(1)} %copy-done), kind=kOutput, calls=%fused_computation.15 | convolution fusion | flops 1032847360 | bytes 17893376 | tf_op jit(solution)/shard_map/lkc,kh->lch/dot_general | solution.py:207
  133.5 8.7 %convert_reduce_fusion = (f32[512]{0:T(512)S(1)}, bf16[8,640,512]{2,1,0:T(8,128)(2,1)S(1)}) fusion(f32[8,640,512]{2,1,0:T(8,128)S(1)} %get-tuple-element.17, f32[512]{0:T(512)S(1)} %copy-done.7, bf16[8,192,640]{2,1,0:T(8,128)(2,1)S(1)} %copy-done.3, bf16[512,192]{0,1:T(8,128)(2,1)S(1)} %copy-done.6), kind=kOutput, calls=%fused_computation.14 | convolution fusion | flops 1066925568 | bytes 17895424 | tf_op jit(solution)/shard_map/lkc,hk->lch/dot_general | solution.py:219
  145.5 4.4 %all-to-all-start.2 = ((bf16[4,8,48,640]{3,2,1,0:T(8,128)(2,1)}), bf16[4,8,48,640]{3,2,1,0:T(8,128)(2,1)}, u32[]{:S(2)}, u32[]{:S(2)}) async-start(bf16[4,8,48,640]{3,2,1,0:T(8,128)(2,1)} %bitcast.105), calls=%async_computation.2 | async-start | bytes 3932160 | tf_op jit(solution)/shard_map/all_to_all | solution.py:244
  150.3 4.4 %convolution_bitcast_fusion.1 = bf16[192,512]{1,0:T(8,128)(2,1)S(1)} fusion(bf16[8,192,640]{2,1,0:T(8,128)(2,1)} %bitcast.115, bf16[8,640,512]{2,1,0:T(8,128)(2,1)} %copy-done.2), kind=kOutput, calls=%fused_computation.31 | convolution fusion | flops 1006632960 | bytes 7405568 | tf_op jit(solution)/shard_map/lkc,lch->kh/dot_general | solution.py:223
  156.0 18.3 %all-to-all-done.2 = bf16[4,8,48,640]{3,2,1,0:T(8,128)(2,1)} async-done(((bf16[4,8,48,640]{3,2,1,0:T(8,128)(2,1)}), bf16[4,8,48,640]{3,2,1,0:T(8,128)(2,1)}, u32[]{:S(2)}, u32[]{:S(2)}) %all-to-all-start.2) | async-done | bytes 1966112 | tf_op jit(solution)/shard_map/all_to_all | solution.py:244
  178.7 18.2 %all_to_all.55 = bf16[32,2,3136]{2,1,0:T(2,128)(2,1)S(1)} all-to-all(bf16[32,2,3136]{2,1,0:T(2,128)(2,1)S(1)} %reshape.143), channel_id=1, replica_groups=mesh['lat'=8,'lon'=4] {'lat','lon'}, dimensions={0} | all-to-all | bytes 802816 | tf_op jit(solution)/shard_map/all_to_all | solution.py:79
  199.4 3.3 %all-to-all-start.5 = ((f32[32,1,6272]{2,1,0:T(1,128)}), f32[32,1,6272]{2,1,0:T(1,128)}, u32[]{:S(2)}, u32[]{:S(2)}) async-start(f32[32,1,6272]{2,1,0:T(1,128)} %broadcast_in_dim.31), calls=%async_computation.5 | async-start | bytes 1605632 | tf_op jit(solution)/shard_map/all_to_all | solution.py:82
  202.8 8.9 %fusion.11 = bf16[1280,8,48,2]{0,2,3,1:T(8,128)(2,1)S(1)} fusion(bf16[2,160,4,8,640]{4,3,2,1,0:T(8,128)(2,1)} %bitcast.106, bf16[4,8,48,640]{3,2,1,0:T(8,128)(2,1)} %all-to-all-done.2), kind=kOutput, calls=%fused_computation.20 | convolution fusion | flops 5034147840 | bytes 17039360 | tf_op jit(solution)/shard_map/cgbn,blkn->glkc/dot_general | solution.py:251
  214.5 6.4 %all_to_all.43 = bf16[8,160,768]{1,0,2:T(8,128)(2,1)S(1)} reshape(bf16[1280,8,48,2]{0,3,2,1:T(2,128)(2,1)} %copy.60) | data formatting | bytes 3932160 | tf_op jit(solution)/shard_map/all_to_all | solution.py:255
  224.2 6.1 %all-to-all-start.3 = ((bf16[8,160,768]{2,1,0:T(8,128)(2,1)}), bf16[8,160,768]{2,1,0:T(8,128)(2,1)S(1)}, u32[]{:S(2)}, u32[]{:S(2)}) async-start(bf16[8,160,768]{2,1,0:T(8,128)(2,1)} %copy.61), calls=%async_computation.3 | async-start | bytes 3932160 | tf_op jit(solution)/shard_map/all_to_all | solution.py:255
  230.3 5.6 %fusion.17 = bf16[8,192,640]{2,1,0:T(8,128)(2,1)} fusion(f32[192]{0:T(256)S(1)} %copy-done.8, bf16[8,640,512]{2,1,0:T(8,128)(2,1)} %get-tuple-element.16, bf16[512,192]{0,1:T(8,128)(2,1)S(1)} %copy-done.6), kind=kOutput, calls=%fused_computation.28 | convolution fusion | flops 1008599040 | bytes 7406336 | tf_op jit(solution)/shard_map/lch,hk->lkc/dot_general | solution.py:212
  244.6 31.3 %all-to-all-done.3 = bf16[8,160,768]{2,1,0:T(8,128)(2,1)S(1)} async-done(((bf16[8,160,768]{2,1,0:T(8,128)(2,1)}), bf16[8,160,768]{2,1,0:T(8,128)(2,1)S(1)}, u32[]{:S(2)}, u32[]{:S(2)}) %all-to-all-start.3) | async-done | bytes 1966112 | tf_op jit(solution)/shard_map/all_to_all | solution.py:255
  278.3 4.6 %reshape.126 = bf16[80,2,64,96]{3,2,1,0:T(8,128)(2,1)S(1)} reshape(bf16[160,8,768]{2,1,0:T(8,128)(2,1)} %copy.62) | data formatting | bytes 3932160 | tf_op jit(solution)/shard_map/reshape | solution.py:256
  285.2 4.2 %copy.63.grad_ref = bf16[80,96,128]{2,1,0:T(8,128)(2,1)} copy(bf16[80,96,128]{1,2,0:T(8,128)(2,1)} %bitcast.109) | data formatting | bytes 3932160 | tf_op jit(solution)/shard_map/reshape | solution.py:259
  289.4 14.8 %shard_map.129 = bf16[80,96,1408]{2,1,0:T(8,128)(2,1)} custom-call(s32[80]{0:T(128)} %dynamic_slice.3.ids_ref, bf16[80,96,128]{2,1,0:T(8,128)(2,1)} %copy.63.grad_ref, bf16[80,32,1408]{2,1,0:T(8,128)(2,1)} %basis_ref.3), custom_call_target="tpu_custom_call" | custom-call | tf_op jit(solution)/shard_map/pallas_call | solution.py:165
  (67 shorter events, 48.7 us)
Async XLA Ops:
  0.6 127.2 %copy-start = (bf16[192,512]{1,0:T(8,128)(2,1)S(1)}, bf16[192,512]{1,0:T(8,128)(2,1)}, u32[]{:S(2)}) copy-start(bf16[192,512]{1,0:T(8,128)(2,1)} %param.11) | copy-start | bytes 589828
  20.0 14.1 %copy-start.5 = (s32[640]{0:T(1024)S(1)}, s32[640]{0:T(1024)}, u32[]{:S(2)}) copy-start(s32[640]{0:T(1024)} %param.8) | copy-start | bytes 7684
  26.3 53.1 %all-to-all-start = ((bf16[160,8,768]{2,0,1:T(8,128)(2,1)}), bf16[160,8,768]{2,0,1:T(8,128)(2,1)S(1)}, u32[]{:S(2)}, u32[]{:S(2)}) async-start(bf16[160,8,768]{2,0,1:T(8,128)(2,1)} %copy.52), calls=%async_computation | async-start | bytes 3932160 | tf_op jit(solution)/shard_map/all_to_all | solution.py:194
  79.5 1.3 copy-start.1
  100.6 27.3 %copy-start.7 = (f32[512]{0:T(512)S(1)}, f32[512]{0:T(512)}, u32[]{:S(2)}) copy-start(f32[512]{0:T(512)} %param.12) | copy-start | bytes 6148
  127.9 5.6 %copy-start.4 = (bf16[8,4,48,640]{3,2,1,0:T(8,128)(2,1)}, bf16[8,4,48,640]{3,2,1,0:T(8,128)(2,1)S(1)}, u32[]{:S(2)}) copy-start(bf16[8,4,48,640]{3,2,1,0:T(8,128)(2,1)S(1)} %copy.56) | copy-start | bytes 5898244
  127.9 5.6 %copy-start.3 = (bf16[8,192,640]{2,1,0:T(8,128)(2,1)S(1)}, bf16[8,192,640]{2,1,0:T(8,128)(2,1)}, u32[]{:S(2)}) copy-start(bf16[8,192,640]{2,1,0:T(8,128)(2,1)} %param.15) | copy-start | bytes 5898244
  127.9 5.6 %copy-start.6 = (bf16[512,192]{0,1:T(8,128)(2,1)S(1)}, bf16[512,192]{0,1:T(8,128)(2,1)}, u32[]{:S(2)}) copy-start(bf16[512,192]{0,1:T(8,128)(2,1)} %param.13) | copy-start | bytes 589828
  142.2 3.3 %copy-start.2 = (bf16[8,640,512]{2,1,0:T(8,128)(2,1)}, bf16[8,640,512]{2,1,0:T(8,128)(2,1)S(1)}, u32[]{:S(2)}) copy-start(bf16[8,640,512]{2,1,0:T(8,128)(2,1)S(1)} %get-tuple-element.19) | copy-start | bytes 15728644
  145.5 28.8 %all-to-all-start.2 = ((bf16[4,8,48,640]{3,2,1,0:T(8,128)(2,1)}), bf16[4,8,48,640]{3,2,1,0:T(8,128)(2,1)}, u32[]{:S(2)}, u32[]{:S(2)}) async-start(bf16[4,8,48,640]{3,2,1,0:T(8,128)(2,1)} %bitcast.105), calls=%async_computation.2 | async-start | bytes 3932160 | tf_op jit(solution)/shard_map/all_to_all | solution.py:244
  149.9 4.8 %slice-start = ((s8[5242880]{0:T(1024)(128)(4,1)}), s8[4194304]{0:T(1024)(128)(4,1)S(1)}, s32[]{:S(2)}) async-start(s8[5242880]{0:T(1024)(128)(4,1)} %bitcast.119), calls=%async_computation.6 | async-start | bytes 8388608
  150.3 4.5 %slice-start.1 = ((s8[5242880]{0:T(1024)(128)(4,1)}), s8[1048576]{0:T(1024)(128)(4,1)S(1)}, s32[]{:S(2)}) async-start(s8[5242880]{0:T(1024)(128)(4,1)} %bitcast.119), calls=%async_computation.7 | async-start | bytes 2097152
  199.4 24.8 %all-to-all-start.5 = ((f32[32,1,6272]{2,1,0:T(1,128)}), f32[32,1,6272]{2,1,0:T(1,128)}, u32[]{:S(2)}, u32[]{:S(2)}) async-start(f32[32,1,6272]{2,1,0:T(1,128)} %broadcast_in_dim.31), calls=%async_computation.5 | async-start | bytes 1605632 | tf_op jit(solution)/shard_map/all_to_all | solution.py:82
  221.0 9.3 %copy-start.8 = (f32[192]{0:T(256)S(1)}, f32[192]{0:T(256)}, u32[]{:S(2)}) copy-start(f32[192]{0:T(256)} %param.14) | copy-start | bytes 2308
  224.2 51.7 %all-to-all-start.3 = ((bf16[8,160,768]{2,1,0:T(8,128)(2,1)}), bf16[8,160,768]{2,1,0:T(8,128)(2,1)S(1)}, u32[]{:S(2)}, u32[]{:S(2)}) async-start(bf16[8,160,768]{2,1,0:T(8,128)(2,1)} %copy.61), calls=%async_computation.3 | async-start | bytes 3932160 | tf_op jit(solution)/shard_map/all_to_all | solution.py:255

commit v5 on v3

--- a/solution.py
+++ b/solution.py
@@ -117,7 +117,10 @@
     step = pl.program_id(0)
     for i in range(block):
         masked_rows(ids_ref, step * block + i, basis_ref[i], rows_ref)
-        out = jnp.dot(grad_ref[i], rows_ref[...], preferred_element_type=jnp.float32)
+        out = lax.dot_general(
+            grad_ref[i], rows_ref[...], (((0,), (0,)), ((), ())),
+            preferred_element_type=jnp.float32,
+        )
         out_ref[i] = out.astype(out_ref.dtype)
 
 
@@ -149,14 +152,14 @@
 
 
 def analysis(local_ids, grads, lat_basis):
-    pairs, width, rows = grads.shape
+    pairs, rows, width = grads.shape
     half, length = lat_basis.shape[1], lat_basis.shape[2]
     block = pair_block(pairs)
     spec = pltpu.PrefetchScalarGridSpec(
         num_scalar_prefetch=1,
         grid=(pairs // block,),
         in_specs=[
-            pl.BlockSpec((block, width, rows), lambda s, ids: (s, 0, 0)),
+            pl.BlockSpec((block, rows, width), lambda s, ids: (s, 0, 0)),
             pl.BlockSpec((block, half, length), lambda s, ids: (s, 0, 0)),
         ],
         out_specs=pl.BlockSpec((block, width, length), lambda s, ids: (s, 0, 0)),
@@ -254,8 +257,8 @@
     pair_grad = lax.all_to_all(flat_grad, "lat", split_axis=0, concat_axis=1, tiled=True)
     pair_grad = pair_grad.reshape(pair_dev, 2, lat_window, width_local)
     pair_grad = jnp.einsum(
-        "lr,pqlk->pkqr", reorder, pair_grad, preferred_element_type=jnp.float32
-    ).astype(jnp.bfloat16).reshape(pair_dev, width_local, 2 * lat_window)
+        "lr,pqlk->pqrk", reorder, pair_grad, preferred_element_type=jnp.float32
+    ).astype(jnp.bfloat16).reshape(pair_dev, 2 * lat_window, width_local)
     spectral_grad = analysis(local_ids, pair_grad, lat_basis)
     return (tendency, spectral_grad, in_weight_grad, in_bias_grad, out_weight_grad, out_bias_grad)
 

time: 309 us -> 306 us (level)
  local copies, waits for them, and re-layouts: 79.1 us -> 74.9 us
    reshape x1 -> x0, local copies, waits for them, and re-layouts: 4.24 us -> none  [per_device(): pair_grad = jnp.einsum('lr,pqlk->pkqr', reorder, pair_grad, preferred_ele...]
where the time goes in v5:
time: 306 us; the launch traced here: 300 us
  waiting for transfers between devices  84.8 us (28%)
  local copies, waits for them, and re-layouts  74.9 us (24%)
  matrix products  49.9 us (16%)
  Pallas kernels  43.5 us (14%)
  starting transfers between devices  29.5 us (10%)
  other arithmetic  16.1 us (5%)
    all_to_all x1, waiting for transfers between devices, per_device(): lax.all_to_all(flat_grad, 'lat', split_axis=0, concat_axis=1, tiled=True)  31.3 us
    all_to_all x1, waiting for transfers between devices, per_device(): level_rows = lax.all_to_all(grad_blocks, 'lon', 0, 0, tiled=True)  23 us
    reshape x1, local copies, waits for them, and re-layouts, per_device(): block_table = full_table.reshape(2, wave_count, lon_parts, block_cols)  23 us
    all_to_all x1, waiting for transfers between devices, per_device(): level_blocks = lax.all_to_all(all_columns, 'lon', 0, 0, tiled=True)  22.3 us
    pallas_call x1, Pallas kernels, analysis(): pl.pallas_call(analyse_kernel, grid_spec=spec, out_shape=jax.ShapeDtypeSt...  15.5 us
    pallas_call x1, Pallas kernels, synthesis(): pl.pallas_call(synth_kernel, grid_spec=spec, out_shape=jax.ShapeDtypeStru...  15.3 us
    pallas_call x1, Pallas kernels, fourier_table(): pl.pallas_call(table_kernel, grid=(count // rows,), in_specs=[pl.BlockSpe...  12.7 us
    all_to_all x3, local copies, waits for them, and re-layouts, per_device(): lax.all_to_all(flat_grad, 'lat', split_axis=0, concat_axis=1, tiled=True)  12 us
  transfers between devices with their start and end apart: 6, of which 6 were waited for; matrix products, arithmetic and copies ran while one was open for 23% of the time, Pallas kernels for 4%

profile of v5, /device:TPU:0, one launch (start us, length us, event | category | flops | bytes accessed | tf_op | source)
XLA Modules:
  0.0 300.0 jit_solution(16077744805696296584)
XLA Ops:
  2.0 15.3 %shard_map.128 = bf16[80,128,96]{2,1,0:T(8,128)(2,1)} custom-call(s32[80]{0:T(128)} %dynamic_slice.3.ids_ref, bf16[80,96,1408]{2,1,0:T(8,128)(2,1)} %spec_ref.1, bf16[80,32,1408]{2,1,0:T(8,128)(2,1)} %basis_ref.3), custom_call_target="tpu_custom_call" | custom-call | tf_op jit(solution)/shard_map/pallas_call | solution.py:147
  26.3 7.8 %all-to-all-start = ((bf16[160,8,768]{2,0,1:T(8,128)(2,1)}), bf16[160,8,768]{2,0,1:T(8,128)(2,1)S(1)}, u32[]{:S(2)}, u32[]{:S(2)}) async-start(bf16[160,8,768]{2,0,1:T(8,128)(2,1)} %copy.49), calls=%async_computation | async-start | bytes 3932160 | tf_op jit(solution)/shard_map/all_to_all | solution.py:197
  36.2 4.0 %fusion.31 = (f32[1280,128]{1,0:T(8,128)}, f32[1280,128]{1,0:T(8,128)}) fusion(s32[1280]{0:T(1024)S(1)} %mul.94), kind=kLoop, calls=%fused_computation.42 | loop fusion | flops 1474560 | bytes 1315840 | tf_op jit(solution)/shard_map/sin | solution.py:50
  43.4 12.7 %shard_map.127 = bf16[2,1280,2560]{2,1,0:T(8,128)(2,1)} custom-call(f32[1280,20]{1,0:T(8,128)} %get-tuple-element.9.cos_a_ref, f32[1280,20]{1,0:T(8,128)} %get-tuple-element.8.sin_a_ref, f32[1280,128]{1,0:T(8,128)} %get-tuple-element.11.cos_b_ref, f32[1280,128]{1,0:T(8,128)} %get-tuple-element.10.sin_b_ref, f32[1280,1]{1,0:T(8,128)} %select_n.46.factor_ref), custom_call_target="tpu_custom_call" | custom-call | tf_op jit(solution)/shard_map/pallas_call | solution.py:56
  56.1 23.0 %reshape.121 = bf16[2,1280,4,640]{3,2,1,0:T(4,128)(2,1)} reshape(bf16[2,1280,2560]{2,1,0:T(8,128)(2,1)} %shard_map.127) | data formatting | bytes 26214400 | tf_op jit(solution)/shard_map/reshape | solution.py:203
  80.7 4.1 %copy.50 = bf16[8,160,768]{1,0,2:T(8,128)(2,1)S(1)} copy(bf16[8,160,768]{2,1,0:T(8,128)(2,1)} %bitcast.115) | data formatting | bytes 3932160 | tf_op jit(solution)/shard_map/all_to_all | solution.py:197
  84.8 5.2 %reshape.123 = bf16[1280,8,48,2]{0,3,2,1:T(2,128)(2,1)} reshape(bf16[8,160,768]{1,0,2:T(8,128)(2,1)S(1)} %copy.50) | data formatting | bytes 3932160 | tf_op jit(solution)/shard_map/reshape | solution.py:199
  90.1 11.8 %fusion.18 = bf16[4,8,48,640]{3,2,1,0:T(8,128)(2,1)} fusion(bf16[1280,8,48,2]{0,3,2,1:T(2,128)(2,1)} %reshape.123, bf16[2,1280,4,640,1]{3,2,1,0,4:T(4,128)(2,1)} %bitcast.111), kind=kOutput, calls=%fused_computation.27 | convolution fusion | flops 5034147840 | bytes 17039360 | tf_op jit(solution)/shard_map/glkc,cgbn->blkn/dot_general | solution.py:204
  101.9 3.9 %all-to-all-start.1 = ((bf16[4,8,48,640]{3,2,1,0:T(8,128)(2,1)}), bf16[4,8,48,640]{3,2,1,0:T(8,128)(2,1)S(1)}, u32[]{:S(2)}, u32[]{:S(2)}) async-start(bf16[4,8,48,640]{3,2,1,0:T(8,128)(2,1)} %fusion.18), calls=%async_computation.1 | async-start | bytes 3932160 | tf_op jit(solution)/shard_map/all_to_all | solution.py:207
  107.7 22.3 %all-to-all-done.1 = bf16[4,8,48,640]{3,2,1,0:T(8,128)(2,1)S(1)} async-done(((bf16[4,8,48,640]{3,2,1,0:T(8,128)(2,1)}), bf16[4,8,48,640]{3,2,1,0:T(8,128)(2,1)S(1)}, u32[]{:S(2)}, u32[]{:S(2)}) %all-to-all-start.1) | async-done | bytes 1966112 | tf_op jit(solution)/shard_map/all_to_all | solution.py:207
  130.3 3.8 %multiply_convert_fusion = (bf16[8,640,512]{2,1,0:T(8,128)(2,1)S(1)}, f32[8,640,512]{2,1,0:T(8,128)S(1)}) fusion(f32[512]{0:T(512)S(1)} %copy-done.6, bf16[8,192,640]{2,1,0:T(8,128)(2,1)S(1)} %bitcast.118, bf16[192,512]{1,0:T(8,128)(2,1)S(1)} %copy-done), kind=kOutput, calls=%fused_computation.14 | convolution fusion | flops 1032847360 | bytes 17893376 | tf_op jit(solution)/shard_map/lkc,kh->lch/dot_general | solution.py:210
  134.1 8.7 %fusion.49 = (bf16[512]{0:T(512)(128)(2,1)S(1)}, bf16[8,640,512]{2,1,0:T(8,128)(2,1)S(1)}) fusion(f32[8,640,512]{2,1,0:T(8,128)S(1)} %get-tuple-element.13, f32[512]{0:T(512)S(1)} %copy-done.6, bf16[8,192,640]{2,1,0:T(8,128)(2,1)S(1)} %copy-done.3, bf16[512,192]{0,1:T(8,128)(2,1)S(1)} %copy-done.5), kind=kOutput, calls=%fused_computation.69 | convolution fusion | flops 1064304128 | bytes 17894400 | tf_op jit(solution)/shard_map/lkc,hk->lch/dot_general | solution.py:222
  151.5 4.9 %all-to-all-start.4 = ((bf16[32,2,3136]{2,1,0:T(2,128)(2,1)}), bf16[32,2,3136]{2,1,0:T(2,128)(2,1)S(1)}, u32[]{:S(2)}, u32[]{:S(2)}) async-start(bf16[32,2,3136]{2,1,0:T(2,128)(2,1)} %reshape.143), calls=%async_computation.4 | async-start | bytes 819200 | tf_op jit(solution)/shard_map/all_to_all | solution.py:79
  156.4 4.3 %convolution_convert_fusion.1 = bf16[8,640,192]{1,2,0:T(8,128)(2,1)S(1)} fusion(bf16[8,640,512]{2,1,0:T(8,128)(2,1)} %copy-done.2, bf16[192,512]{1,0:T(8,128)(2,1)S(1)} %copy-done), kind=kOutput, calls=%fused_computation.25 | convolution fusion | flops 1007616000 | bytes 7405568 | tf_op jit(solution)/shard_map/lch,kh->lkc/dot_general | solution.py:228
  162.2 7.7 %all-to-all-done.4 = bf16[32,2,3136]{2,1,0:T(2,128)(2,1)S(1)} async-done(((bf16[32,2,3136]{2,1,0:T(2,128)(2,1)}), bf16[32,2,3136]{2,1,0:T(2,128)(2,1)S(1)}, u32[]{:S(2)}, u32[]{:S(2)}) %all-to-all-start.4) | async-done | bytes 401440 | tf_op jit(solution)/shard_map/all_to_all | solution.py:79
  169.9 3.6 %all-to-all-start.2 = ((bf16[4,8,48,640]{3,2,1,0:T(8,128)(2,1)}), bf16[4,8,48,640]{3,2,1,0:T(8,128)(2,1)S(1)}, u32[]{:S(2)}, u32[]{:S(2)}) async-start(bf16[4,8,48,640]{3,2,1,0:T(8,128)(2,1)} %bitcast.109), calls=%async_computation.2 | async-start | bytes 3932160 | tf_op jit(solution)/shard_map/all_to_all | solution.py:252
  174.8 23.0 %all-to-all-done.2 = bf16[4,8,48,640]{3,2,1,0:T(8,128)(2,1)S(1)} async-done(((bf16[4,8,48,640]{3,2,1,0:T(8,128)(2,1)}), bf16[4,8,48,640]{3,2,1,0:T(8,128)(2,1)S(1)}, u32[]{:S(2)}, u32[]{:S(2)}) %all-to-all-start.2) | async-done | bytes 1966112 | tf_op jit(solution)/shard_map/all_to_all | solution.py:252
  202.4 8.4 %fusion.11 = bf16[1280,8,48,2]{0,2,3,1:T(8,128)(2,1)S(1)} fusion(bf16[2,160,4,8,640]{4,3,2,1,0:T(8,128)(2,1)} %bitcast.110, bf16[4,8,48,640]{3,2,1,0:T(8,128)(2,1)S(1)} %all-to-all-done.2), kind=kOutput, calls=%fused_computation.18 | convolution fusion | flops 5034147840 | bytes 17039360 | tf_op jit(solution)/shard_map/cgbn,blkn->glkc/dot_general | solution.py:253
  213.6 6.4 %all_to_all.43 = bf16[8,160,768]{1,0,2:T(8,128)(2,1)S(1)} reshape(bf16[1280,8,48,2]{0,3,2,1:T(2,128)(2,1)} %copy.57) | data formatting | bytes 3932160 | tf_op jit(solution)/shard_map/all_to_all | solution.py:257
  223.4 6.0 %all-to-all-start.3 = ((bf16[8,160,768]{2,1,0:T(8,128)(2,1)}), bf16[8,160,768]{2,1,0:T(8,128)(2,1)S(1)}, u32[]{:S(2)}, u32[]{:S(2)}) async-start(bf16[8,160,768]{2,1,0:T(8,128)(2,1)} %copy.58), calls=%async_computation.3 | async-start | bytes 3932160 | tf_op jit(solution)/shard_map/all_to_all | solution.py:257
  229.3 5.6 %fusion.17 = bf16[8,192,640]{2,1,0:T(8,128)(2,1)} fusion(f32[192]{0:T(256)S(1)} %copy-done.7, bf16[8,640,512]{2,1,0:T(8,128)(2,1)} %copy-done.8, bf16[512,192]{0,1:T(8,128)(2,1)} %param.13), kind=kOutput, calls=%fused_computation.26 | convolution fusion | flops 1008599040 | bytes 7406336 | tf_op jit(solution)/shard_map/lch,hk->lkc/dot_general | solution.py:215
  243.7 31.3 %all-to-all-done.3 = bf16[8,160,768]{2,1,0:T(8,128)(2,1)S(1)} async-done(((bf16[8,160,768]{2,1,0:T(8,128)(2,1)}), bf16[8,160,768]{2,1,0:T(8,128)(2,1)S(1)}, u32[]{:S(2)}, u32[]{:S(2)}) %all-to-all-start.3) | async-done | bytes 1966112 | tf_op jit(solution)/shard_map/all_to_all | solution.py:257
  277.4 4.6 %reshape.126 = bf16[80,2,64,96]{3,2,1,0:T(8,128)(2,1)S(1)} reshape(bf16[160,8,768]{2,1,0:T(8,128)(2,1)} %copy.59) | data formatting | bytes 3932160 | tf_op jit(solution)/shard_map/reshape | solution.py:258
  284.3 15.5 %shard_map.129 = bf16[80,96,1408]{2,1,0:T(8,128)(2,1)} custom-call(s32[80]{0:T(128)} %dynamic_slice.3.ids_ref, bf16[80,128,96]{2,1,0:T(8,128)(2,1)} %bitcast.112, bf16[80,32,1408]{2,1,0:T(8,128)(2,1)} %basis_ref.3), custom_call_target="tpu_custom_call" | custom-call | tf_op jit(solution)/shard_map/pallas_call | solution.py:168
  (65 shorter events, 54.9 us)
Async XLA Ops:
  0.6 129.6 %copy-start = (bf16[192,512]{1,0:T(8,128)(2,1)S(1)}, bf16[192,512]{1,0:T(8,128)(2,1)}, u32[]{:S(2)}) copy-start(bf16[192,512]{1,0:T(8,128)(2,1)} %param.11) | copy-start | bytes 589828
  20.0 14.1 %copy-start.4 = (s32[640]{0:T(1024)S(1)}, s32[640]{0:T(1024)}, u32[]{:S(2)}) copy-start(s32[640]{0:T(1024)} %param.8) | copy-start | bytes 7684
  26.3 53.1 %all-to-all-start = ((bf16[160,8,768]{2,0,1:T(8,128)(2,1)}), bf16[160,8,768]{2,0,1:T(8,128)(2,1)S(1)}, u32[]{:S(2)}, u32[]{:S(2)}) async-start(bf16[160,8,768]{2,0,1:T(8,128)(2,1)} %copy.49), calls=%async_computation | async-start | bytes 3932160 | tf_op jit(solution)/shard_map/all_to_all | solution.py:197
  79.5 1.3 copy-start.1
  101.9 28.4 %copy-start.6 = (f32[512]{0:T(512)S(1)}, f32[512]{0:T(512)}, u32[]{:S(2)}) copy-start(f32[512]{0:T(512)} %param.12) | copy-start | bytes 6148
  101.9 28.2 %all-to-all-start.1 = ((bf16[4,8,48,640]{3,2,1,0:T(8,128)(2,1)}), bf16[4,8,48,640]{3,2,1,0:T(8,128)(2,1)S(1)}, u32[]{:S(2)}, u32[]{:S(2)}) async-start(bf16[4,8,48,640]{3,2,1,0:T(8,128)(2,1)} %fusion.18), calls=%async_computation.1 | async-start | bytes 3932160 | tf_op jit(solution)/shard_map/all_to_all | solution.py:207
  130.3 3.8 %copy-start.3 = (bf16[8,192,640]{2,1,0:T(8,128)(2,1)S(1)}, bf16[8,192,640]{2,1,0:T(8,128)(2,1)}, u32[]{:S(2)}) copy-start(bf16[8,192,640]{2,1,0:T(8,128)(2,1)} %param.15) | copy-start | bytes 5898244
  130.3 3.8 %copy-start.5 = (bf16[512,192]{0,1:T(8,128)(2,1)S(1)}, bf16[512,192]{0,1:T(8,128)(2,1)}, u32[]{:S(2)}) copy-start(bf16[512,192]{0,1:T(8,128)(2,1)} %param.13) | copy-start | bytes 589828
  134.1 11.1 %copy-start.8 = (bf16[8,640,512]{2,1,0:T(8,128)(2,1)}, bf16[8,640,512]{2,1,0:T(8,128)(2,1)S(1)}, u32[]{:S(2)}) copy-start(bf16[8,640,512]{2,1,0:T(8,128)(2,1)S(1)} %get-tuple-element.12) | copy-start | bytes 15728644
  142.8 2.3 copy-start.2
  151.5 18.4 %all-to-all-start.4 = ((bf16[32,2,3136]{2,1,0:T(2,128)(2,1)}), bf16[32,2,3136]{2,1,0:T(2,128)(2,1)S(1)}, u32[]{:S(2)}, u32[]{:S(2)}) async-start(bf16[32,2,3136]{2,1,0:T(2,128)(2,1)} %reshape.143), calls=%async_computation.4 | async-start | bytes 819200 | tf_op jit(solution)/shard_map/all_to_all | solution.py:79
  169.9 27.9 %all-to-all-start.2 = ((bf16[4,8,48,640]{3,2,1,0:T(8,128)(2,1)}), bf16[4,8,48,640]{3,2,1,0:T(8,128)(2,1)S(1)}, u32[]{:S(2)}, u32[]{:S(2)}) async-start(bf16[4,8,48,640]{3,2,1,0:T(8,128)(2,1)} %bitcast.109), calls=%async_computation.2 | async-start | bytes 3932160 | tf_op jit(solution)/shard_map/all_to_all | solution.py:252
  199.1 24.3 %all-to-all-start.5 = ((f32[32,1,6272]{2,1,0:T(1,128)}), f32[32,1,6272]{2,1,0:T(1,128)}, u32[]{:S(2)}, u32[]{:S(2)}) async-start(f32[32,1,6272]{2,1,0:T(1,128)} %broadcast_in_dim.33), calls=%async_computation.5 | async-start | bytes 1605632 | tf_op jit(solution)/shard_map/all_to_all | solution.py:82
  220.0 9.3 %copy-start.7 = (f32[192]{0:T(256)S(1)}, f32[192]{0:T(256)}, u32[]{:S(2)}) copy-start(f32[192]{0:T(256)} %param.14) | copy-start | bytes 2308
  223.4 51.7 %all-to-all-start.3 = ((bf16[8,160,768]{2,1,0:T(8,128)(2,1)}), bf16[8,160,768]{2,1,0:T(8,128)(2,1)S(1)}, u32[]{:S(2)}, u32[]{:S(2)}) async-start(bf16[8,160,768]{2,1,0:T(8,128)(2,1)} %copy.58), calls=%async_computation.3 | async-start | bytes 3932160 | tf_op jit(solution)/shard_map/all_to_all | solution.py:257

commit v6 on v5

--- a/solution.py
+++ b/solution.py
@@ -125,7 +125,7 @@
 
 
 def pair_block(count):
-    for size in (16, 8, 4, 2, 1):
+    for size in (20, 16, 8, 4, 2, 1):
         if count % size == 0:
             return size
 

time: 306 us -> 305 us (level)
  no operation moved by 1% of the time
where the time goes in v6:
time: 305 us; the launch traced here: 299 us
  waiting for transfers between devices  84.9 us (28%)
  local copies, waits for them, and re-layouts  74.9 us (25%)
  matrix products  49.9 us (16%)
  Pallas kernels  42.4 us (14%)
  starting transfers between devices  29.5 us (10%)
  other arithmetic  16.1 us (5%)
    all_to_all x1, waiting for transfers between devices, per_device(): lax.all_to_all(flat_grad, 'lat', split_axis=0, concat_axis=1, tiled=True)  31.3 us
    all_to_all x1, waiting for transfers between devices, per_device(): level_rows = lax.all_to_all(grad_blocks, 'lon', 0, 0, tiled=True)  23 us
    reshape x1, local copies, waits for them, and re-layouts, per_device(): block_table = full_table.reshape(2, wave_count, lon_parts, block_cols)  23 us
    all_to_all x1, waiting for transfers between devices, per_device(): level_blocks = lax.all_to_all(all_columns, 'lon', 0, 0, tiled=True)  22.3 us
    pallas_call x1, Pallas kernels, analysis(): pl.pallas_call(analyse_kernel, grid_spec=spec, out_shape=jax.ShapeDtypeSt...  15 us
    pallas_call x1, Pallas kernels, synthesis(): pl.pallas_call(synth_kernel, grid_spec=spec, out_shape=jax.ShapeDtypeStru...  14.6 us
    pallas_call x1, Pallas kernels, fourier_table(): pl.pallas_call(table_kernel, grid=(count // rows,), in_specs=[pl.BlockSpe...  12.7 us
    all_to_all x3, local copies, waits for them, and re-layouts, per_device(): lax.all_to_all(flat_grad, 'lat', split_axis=0, concat_axis=1, tiled=True)  12 us
  transfers between devices with their start and end apart: 6, of which 6 were waited for; matrix products, arithmetic and copies ran while one was open for 23% of the time, Pallas kernels for 4%

profile of v6, /device:TPU:0, one launch (start us, length us, event | category | flops | bytes accessed | tf_op | source)
XLA Modules:
  0.0 298.9 jit_solution(16576692772948815116)
XLA Ops:
  2.0 14.6 %shard_map.128 = bf16[80,128,96]{2,1,0:T(8,128)(2,1)} custom-call(s32[80]{0:T(128)} %dynamic_slice.3.ids_ref, bf16[80,96,1408]{2,1,0:T(8,128)(2,1)} %spec_ref.1, bf16[80,32,1408]{2,1,0:T(8,128)(2,1)} %basis_ref.3), custom_call_target="tpu_custom_call" | custom-call | tf_op jit(solution)/shard_map/pallas_call | solution.py:147
  25.7 7.8 %all-to-all-start = ((bf16[160,8,768]{2,0,1:T(8,128)(2,1)}), bf16[160,8,768]{2,0,1:T(8,128)(2,1)S(1)}, u32[]{:S(2)}, u32[]{:S(2)}) async-start(bf16[160,8,768]{2,0,1:T(8,128)(2,1)} %copy.49), calls=%async_computation | async-start | bytes 3932160 | tf_op jit(solution)/shard_map/all_to_all | solution.py:197
  35.6 4.0 %fusion.31 = (f32[1280,128]{1,0:T(8,128)}, f32[1280,128]{1,0:T(8,128)}) fusion(s32[1280]{0:T(1024)S(1)} %mul.94), kind=kLoop, calls=%fused_computation.42 | loop fusion | flops 1474560 | bytes 1315840 | tf_op jit(solution)/shard_map/sin | solution.py:50
  42.8 12.7 %shard_map.127 = bf16[2,1280,2560]{2,1,0:T(8,128)(2,1)} custom-call(f32[1280,20]{1,0:T(8,128)} %get-tuple-element.9.cos_a_ref, f32[1280,20]{1,0:T(8,128)} %get-tuple-element.8.sin_a_ref, f32[1280,128]{1,0:T(8,128)} %get-tuple-element.11.cos_b_ref, f32[1280,128]{1,0:T(8,128)} %get-tuple-element.10.sin_b_ref, f32[1280,1]{1,0:T(8,128)} %select_n.46.factor_ref), custom_call_target="tpu_custom_call" | custom-call | tf_op jit(solution)/shard_map/pallas_call | solution.py:56
  55.5 23.0 %reshape.121 = bf16[2,1280,4,640]{3,2,1,0:T(4,128)(2,1)} reshape(bf16[2,1280,2560]{2,1,0:T(8,128)(2,1)} %shard_map.127) | data formatting | bytes 26214400 | tf_op jit(solution)/shard_map/reshape | solution.py:203
  80.1 4.1 %copy.50 = bf16[8,160,768]{1,0,2:T(8,128)(2,1)S(1)} copy(bf16[8,160,768]{2,1,0:T(8,128)(2,1)} %bitcast.115) | data formatting | bytes 3932160 | tf_op jit(solution)/shard_map/all_to_all | solution.py:197
  84.2 5.2 %reshape.123 = bf16[1280,8,48,2]{0,3,2,1:T(2,128)(2,1)} reshape(bf16[8,160,768]{1,0,2:T(8,128)(2,1)S(1)} %copy.50) | data formatting | bytes 3932160 | tf_op jit(solution)/shard_map/reshape | solution.py:199
  89.5 11.8 %fusion.18 = bf16[4,8,48,640]{3,2,1,0:T(8,128)(2,1)} fusion(bf16[1280,8,48,2]{0,3,2,1:T(2,128)(2,1)} %reshape.123, bf16[2,1280,4,640,1]{3,2,1,0,4:T(4,128)(2,1)} %bitcast.111), kind=kOutput, calls=%fused_computation.27 | convolution fusion | flops 5034147840 | bytes 17039360 | tf_op jit(solution)/shard_map/glkc,cgbn->blkn/dot_general | solution.py:204
  101.3 3.9 %all-to-all-start.1 = ((bf16[4,8,48,640]{3,2,1,0:T(8,128)(2,1)}), bf16[4,8,48,640]{3,2,1,0:T(8,128)(2,1)S(1)}, u32[]{:S(2)}, u32[]{:S(2)}) async-start(bf16[4,8,48,640]{3,2,1,0:T(8,128)(2,1)} %fusion.18), calls=%async_computation.1 | async-start | bytes 3932160 | tf_op jit(solution)/shard_map/all_to_all | solution.py:207
  107.1 22.3 %all-to-all-done.1 = bf16[4,8,48,640]{3,2,1,0:T(8,128)(2,1)S(1)} async-done(((bf16[4,8,48,640]{3,2,1,0:T(8,128)(2,1)}), bf16[4,8,48,640]{3,2,1,0:T(8,128)(2,1)S(1)}, u32[]{:S(2)}, u32[]{:S(2)}) %all-to-all-start.1) | async-done | bytes 1966112 | tf_op jit(solution)/shard_map/all_to_all | solution.py:207
  129.7 3.8 %multiply_convert_fusion = (bf16[8,640,512]{2,1,0:T(8,128)(2,1)S(1)}, f32[8,640,512]{2,1,0:T(8,128)S(1)}) fusion(f32[512]{0:T(512)S(1)} %copy-done.6, bf16[8,192,640]{2,1,0:T(8,128)(2,1)S(1)} %bitcast.118, bf16[192,512]{1,0:T(8,128)(2,1)S(1)} %copy-done), kind=kOutput, calls=%fused_computation.14 | convolution fusion | flops 1032847360 | bytes 17893376 | tf_op jit(solution)/shard_map/lkc,kh->lch/dot_general | solution.py:210
  133.5 8.7 %fusion.49 = (bf16[512]{0:T(512)(128)(2,1)S(1)}, bf16[8,640,512]{2,1,0:T(8,128)(2,1)S(1)}) fusion(f32[8,640,512]{2,1,0:T(8,128)S(1)} %get-tuple-element.13, f32[512]{0:T(512)S(1)} %copy-done.6, bf16[8,192,640]{2,1,0:T(8,128)(2,1)S(1)} %copy-done.3, bf16[512,192]{0,1:T(8,128)(2,1)S(1)} %copy-done.5), kind=kOutput, calls=%fused_computation.69 | convolution fusion | flops 1064304128 | bytes 17894400 | tf_op jit(solution)/shard_map/lkc,hk->lch/dot_general | solution.py:222
  150.9 4.9 %all-to-all-start.4 = ((bf16[32,2,3136]{2,1,0:T(2,128)(2,1)}), bf16[32,2,3136]{2,1,0:T(2,128)(2,1)S(1)}, u32[]{:S(2)}, u32[]{:S(2)}) async-start(bf16[32,2,3136]{2,1,0:T(2,128)(2,1)} %reshape.143), calls=%async_computation.4 | async-start | bytes 819200 | tf_op jit(solution)/shard_map/all_to_all | solution.py:79
  155.8 4.3 %convolution_convert_fusion.1 = bf16[8,640,192]{1,2,0:T(8,128)(2,1)S(1)} fusion(bf16[8,640,512]{2,1,0:T(8,128)(2,1)} %copy-done.2, bf16[192,512]{1,0:T(8,128)(2,1)S(1)} %copy-done), kind=kOutput, calls=%fused_computation.25 | convolution fusion | flops 1007616000 | bytes 7405568 | tf_op jit(solution)/shard_map/lch,kh->lkc/dot_general | solution.py:228
  161.6 7.7 %all-to-all-done.4 = bf16[32,2,3136]{2,1,0:T(2,128)(2,1)S(1)} async-done(((bf16[32,2,3136]{2,1,0:T(2,128)(2,1)}), bf16[32,2,3136]{2,1,0:T(2,128)(2,1)S(1)}, u32[]{:S(2)}, u32[]{:S(2)}) %all-to-all-start.4) | async-done | bytes 401440 | tf_op jit(solution)/shard_map/all_to_all | solution.py:79
  169.2 3.6 %all-to-all-start.2 = ((bf16[4,8,48,640]{3,2,1,0:T(8,128)(2,1)}), bf16[4,8,48,640]{3,2,1,0:T(8,128)(2,1)S(1)}, u32[]{:S(2)}, u32[]{:S(2)}) async-start(bf16[4,8,48,640]{3,2,1,0:T(8,128)(2,1)} %bitcast.109), calls=%async_computation.2 | async-start | bytes 3932160 | tf_op jit(solution)/shard_map/all_to_all | solution.py:252
  174.1 23.0 %all-to-all-done.2 = bf16[4,8,48,640]{3,2,1,0:T(8,128)(2,1)S(1)} async-done(((bf16[4,8,48,640]{3,2,1,0:T(8,128)(2,1)}), bf16[4,8,48,640]{3,2,1,0:T(8,128)(2,1)S(1)}, u32[]{:S(2)}, u32[]{:S(2)}) %all-to-all-start.2) | async-done | bytes 1966112 | tf_op jit(solution)/shard_map/all_to_all | solution.py:252
  201.8 8.4 %fusion.11 = bf16[1280,8,48,2]{0,2,3,1:T(8,128)(2,1)S(1)} fusion(bf16[2,160,4,8,640]{4,3,2,1,0:T(8,128)(2,1)} %bitcast.110, bf16[4,8,48,640]{3,2,1,0:T(8,128)(2,1)S(1)} %all-to-all-done.2), kind=kOutput, calls=%fused_computation.18 | convolution fusion | flops 5034147840 | bytes 17039360 | tf_op jit(solution)/shard_map/cgbn,blkn->glkc/dot_general | solution.py:253
  212.9 6.4 %all_to_all.43 = bf16[8,160,768]{1,0,2:T(8,128)(2,1)S(1)} reshape(bf16[1280,8,48,2]{0,3,2,1:T(2,128)(2,1)} %copy.57) | data formatting | bytes 3932160 | tf_op jit(solution)/shard_map/all_to_all | solution.py:257
  222.7 6.0 %all-to-all-start.3 = ((bf16[8,160,768]{2,1,0:T(8,128)(2,1)}), bf16[8,160,768]{2,1,0:T(8,128)(2,1)S(1)}, u32[]{:S(2)}, u32[]{:S(2)}) async-start(bf16[8,160,768]{2,1,0:T(8,128)(2,1)} %copy.58), calls=%async_computation.3 | async-start | bytes 3932160 | tf_op jit(solution)/shard_map/all_to_all | solution.py:257
  228.7 5.6 %fusion.17 = bf16[8,192,640]{2,1,0:T(8,128)(2,1)} fusion(f32[192]{0:T(256)S(1)} %copy-done.7, bf16[8,640,512]{2,1,0:T(8,128)(2,1)} %copy-done.8, bf16[512,192]{0,1:T(8,128)(2,1)} %param.13), kind=kOutput, calls=%fused_computation.26 | convolution fusion | flops 1008599040 | bytes 7406336 | tf_op jit(solution)/shard_map/lch,hk->lkc/dot_general | solution.py:215
  243.0 31.3 %all-to-all-done.3 = bf16[8,160,768]{2,1,0:T(8,128)(2,1)S(1)} async-done(((bf16[8,160,768]{2,1,0:T(8,128)(2,1)}), bf16[8,160,768]{2,1,0:T(8,128)(2,1)S(1)}, u32[]{:S(2)}, u32[]{:S(2)}) %all-to-all-start.3) | async-done | bytes 1966112 | tf_op jit(solution)/shard_map/all_to_all | solution.py:257
  276.7 4.6 %reshape.126 = bf16[80,2,64,96]{3,2,1,0:T(8,128)(2,1)S(1)} reshape(bf16[160,8,768]{2,1,0:T(8,128)(2,1)} %copy.59) | data formatting | bytes 3932160 | tf_op jit(solution)/shard_map/reshape | solution.py:258
  283.6 15.0 %shard_map.129 = bf16[80,96,1408]{2,1,0:T(8,128)(2,1)} custom-call(s32[80]{0:T(128)} %dynamic_slice.3.ids_ref, bf16[80,128,96]{2,1,0:T(8,128)(2,1)} %bitcast.112, bf16[80,32,1408]{2,1,0:T(8,128)(2,1)} %basis_ref.3), custom_call_target="tpu_custom_call" | custom-call | tf_op jit(solution)/shard_map/pallas_call | solution.py:168
  (65 shorter events, 54.9 us)
Async XLA Ops:
  0.6 129.0 %copy-start = (bf16[192,512]{1,0:T(8,128)(2,1)S(1)}, bf16[192,512]{1,0:T(8,128)(2,1)}, u32[]{:S(2)}) copy-start(bf16[192,512]{1,0:T(8,128)(2,1)} %param.11) | copy-start | bytes 589828
  19.3 14.2 %copy-start.4 = (s32[640]{0:T(1024)S(1)}, s32[640]{0:T(1024)}, u32[]{:S(2)}) copy-start(s32[640]{0:T(1024)} %param.8) | copy-start | bytes 7684
  25.7 53.2 %all-to-all-start = ((bf16[160,8,768]{2,0,1:T(8,128)(2,1)}), bf16[160,8,768]{2,0,1:T(8,128)(2,1)S(1)}, u32[]{:S(2)}, u32[]{:S(2)}) async-start(bf16[160,8,768]{2,0,1:T(8,128)(2,1)} %copy.49), calls=%async_computation | async-start | bytes 3932160 | tf_op jit(solution)/shard_map/all_to_all | solution.py:197
  78.9 1.3 copy-start.1
  101.3 28.4 %copy-start.6 = (f32[512]{0:T(512)S(1)}, f32[512]{0:T(512)}, u32[]{:S(2)}) copy-start(f32[512]{0:T(512)} %param.12) | copy-start | bytes 6148
  101.3 28.2 %all-to-all-start.1 = ((bf16[4,8,48,640]{3,2,1,0:T(8,128)(2,1)}), bf16[4,8,48,640]{3,2,1,0:T(8,128)(2,1)S(1)}, u32[]{:S(2)}, u32[]{:S(2)}) async-start(bf16[4,8,48,640]{3,2,1,0:T(8,128)(2,1)} %fusion.18), calls=%async_computation.1 | async-start | bytes 3932160 | tf_op jit(solution)/shard_map/all_to_all | solution.py:207
  129.6 3.8 %copy-start.3 = (bf16[8,192,640]{2,1,0:T(8,128)(2,1)S(1)}, bf16[8,192,640]{2,1,0:T(8,128)(2,1)}, u32[]{:S(2)}) copy-start(bf16[8,192,640]{2,1,0:T(8,128)(2,1)} %param.15) | copy-start | bytes 5898244
  129.7 3.8 %copy-start.5 = (bf16[512,192]{0,1:T(8,128)(2,1)S(1)}, bf16[512,192]{0,1:T(8,128)(2,1)}, u32[]{:S(2)}) copy-start(bf16[512,192]{0,1:T(8,128)(2,1)} %param.13) | copy-start | bytes 589828
  133.5 11.1 %copy-start.8 = (bf16[8,640,512]{2,1,0:T(8,128)(2,1)}, bf16[8,640,512]{2,1,0:T(8,128)(2,1)S(1)}, u32[]{:S(2)}) copy-start(bf16[8,640,512]{2,1,0:T(8,128)(2,1)S(1)} %get-tuple-element.12) | copy-start | bytes 15728644
  142.2 2.3 copy-start.2
  150.9 18.3 %all-to-all-start.4 = ((bf16[32,2,3136]{2,1,0:T(2,128)(2,1)}), bf16[32,2,3136]{2,1,0:T(2,128)(2,1)S(1)}, u32[]{:S(2)}, u32[]{:S(2)}) async-start(bf16[32,2,3136]{2,1,0:T(2,128)(2,1)} %reshape.143), calls=%async_computation.4 | async-start | bytes 819200 | tf_op jit(solution)/shard_map/all_to_all | solution.py:79
  169.2 27.9 %all-to-all-start.2 = ((bf16[4,8,48,640]{3,2,1,0:T(8,128)(2,1)}), bf16[4,8,48,640]{3,2,1,0:T(8,128)(2,1)S(1)}, u32[]{:S(2)}, u32[]{:S(2)}) async-start(bf16[4,8,48,640]{3,2,1,0:T(8,128)(2,1)} %bitcast.109), calls=%async_computation.2 | async-start | bytes 3932160 | tf_op jit(solution)/shard_map/all_to_all | solution.py:252
  198.4 24.3 %all-to-all-start.5 = ((f32[32,1,6272]{2,1,0:T(1,128)}), f32[32,1,6272]{2,1,0:T(1,128)}, u32[]{:S(2)}, u32[]{:S(2)}) async-start(f32[32,1,6272]{2,1,0:T(1,128)} %broadcast_in_dim.33), calls=%async_computation.5 | async-start | bytes 1605632 | tf_op jit(solution)/shard_map/all_to_all | solution.py:82
  219.4 9.3 %copy-start.7 = (f32[192]{0:T(256)S(1)}, f32[192]{0:T(256)}, u32[]{:S(2)}) copy-start(f32[192]{0:T(256)} %param.14) | copy-start | bytes 2308
  222.7 51.7 %all-to-all-start.3 = ((bf16[8,160,768]{2,1,0:T(8,128)(2,1)}), bf16[8,160,768]{2,1,0:T(8,128)(2,1)S(1)}, u32[]{:S(2)}, u32[]{:S(2)}) async-start(bf16[8,160,768]{2,1,0:T(8,128)(2,1)} %copy.58), calls=%async_computation.3 | async-start | bytes 3932160 | tf_op jit(solution)/shard_map/all_to_all | solution.py:257
